TPU v7x, 32 devices: a whole 2x2x4 slice. The times are simulated.
32 devices in a mesh: row: 8 (over y, x, core), col: 4 (over z).
Axes of the slice: x: 2, y: 2, z: 4, core: 2. Of those that a mesh axis runs over, the one named last changes fastest.
Arguments:
- latents: bfloat16 [256, 64, 1024], P('row', 'col'), may hold values from -6 to 6
- row_qkv: bfloat16 [1024, 3072], replicated, may hold values from -2 to 2, as said below
- row_out: bfloat16 [1024, 1024], replicated, may hold values from -0.75 to 0.75
- col_qkv: bfloat16 [1024, 3072], replicated, may hold values from -2 to 2, as said below
- col_out: bfloat16 [1024, 1024], replicated, may hold values from -0.75 to 0.75
- up_weight: bfloat16 [1024, 2048], replicated, may hold values from -0.1875 to 0.1875
- down_weight: bfloat16 [2048, 1024], replicated, may hold values from -0.25 to 0.25
Outputs:
- result: bfloat16 [256, 64, 1024], P('row', 'col')
Inputs may be any that keep to these rules, and one draw needn't show every extreme that they name: `row_qkv`: a projection matrix. `col_qkv`: a projection matrix.
All inputs are finite; a program needn't handle non-finite values.
Results may differ from a plain program's by a relative error of at most 0.02.
Values may be sent and summed in bfloat16 or wider, within the bound.
No kernel may reach another device: no remote copies, remote signals or barrier semaphores. Data moves between devices by JAX's collectives and lax.ppermute only.
A program may use at most 192 MiB of HBM per device.

v0:
```python
import jax
import jax.numpy as jnp
from jax import lax
from jax.sharding import PartitionSpec as P

HEADS = 8


def normalize(values):
    wide = values.astype(jnp.float32)
    return (wide * lax.rsqrt(jnp.mean(wide * wide, -1, keepdims=True) + 1e-06)).astype(jnp.bfloat16)


def project(normed, weight):
    rows, cols, width = normed.shape
    flat = jnp.dot(normed.reshape(rows * cols, width), weight, preferred_element_type=jnp.float32)
    return flat.astype(jnp.bfloat16).reshape(rows, cols, 3, HEADS, width // HEADS)


def attend_rows(query, keys, values):
    scale = 1.0 / query.shape[-1] ** 0.5
    scores = jnp.einsum("aqhd,akhd->ahqk", query, keys, preferred_element_type=jnp.float32) * scale
    probs = jax.nn.softmax(scores, -1).astype(jnp.bfloat16)
    return jnp.einsum("ahqk,akhd->aqhd", probs, values, preferred_element_type=jnp.float32).astype(
        jnp.bfloat16
    )


def attend_cols(query, keys, values):
    scale = 1.0 / query.shape[-1] ** 0.5
    scores = jnp.einsum("qbhd,kbhd->bhqk", query, keys, preferred_element_type=jnp.float32) * scale
    probs = jax.nn.softmax(scores, -1).astype(jnp.bfloat16)
    return jnp.einsum("bhqk,kbhd->qbhd", probs, values, preferred_element_type=jnp.float32).astype(
        jnp.bfloat16
    )


def row_heads(block):
    return attend_rows(block[:, :, 0], block[:, :, 1], block[:, :, 2])


def col_heads(block):
    return attend_cols(block[:, :, 0], block[:, :, 1], block[:, :, 2])


def add_projected(base, mixed, weight):
    rows, cols, width = base.shape
    term = jnp.dot(
        mixed.reshape(rows * cols, width), weight, preferred_element_type=jnp.float32
    ).reshape(rows, cols, width)
    return (base.astype(jnp.float32) + term).astype(jnp.bfloat16)


def feed_forward(after2, up_weight, down_weight):
    rows, cols, width = after2.shape
    normed3 = normalize(after2).reshape(rows * cols, width)
    hidden = jax.nn.gelu(
        jnp.dot(normed3, up_weight, preferred_element_type=jnp.float32), approximate=True
    ).astype(jnp.bfloat16)
    term = jnp.dot(hidden, down_weight, preferred_element_type=jnp.float32).reshape(
        rows, cols, width
    )
    return (after2.astype(jnp.float32) + term).astype(jnp.bfloat16)


def on_device(latents, row_qkv, row_out, col_qkv, col_out, up_weight, down_weight):
    full_rows = lax.all_to_all(latents, "col", split_axis=0, concat_axis=1, tiled=True)
    proj1 = project(normalize(full_rows), row_qkv)
    mixed1 = row_heads(proj1)
    after1 = add_projected(full_rows, mixed1, row_out)
    full_cols = lax.all_to_all(after1, ("row", "col"), split_axis=1, concat_axis=0, tiled=True)
    proj2 = project(normalize(full_cols), col_qkv)
    mixed2 = col_heads(proj2)
    after2 = add_projected(full_cols, mixed2, col_out)
    output = feed_forward(after2, up_weight, down_weight)
    back_rows = lax.all_to_all(output, ("row", "col"), split_axis=0, concat_axis=1, tiled=True)
    return lax.all_to_all(back_rows, "col", split_axis=1, concat_axis=0, tiled=True)


def solution(mesh):
    in_specs = (P("row", "col", None), P(), P(), P(), P(), P(), P())
    out_specs = P("row", "col", None)
    return jax.shard_map(
        on_device, mesh=mesh, in_specs=in_specs, out_specs=out_specs, check_vma=False
    )
```

profile of v0, /device:TPU:0, one launch (start us, length us, event | category | flops | bytes accessed | tf_op | source)
XLA Modules:
  0.0 192.2 jit_solution(5446489298587127472)
XLA Ops:
  0.0 32.2 %all_to_all.54 = bf16[32,16,1024]{2,1,0:T(8,128)(2,1)S(1)} all-to-all(bf16[32,16,1024]{2,1,0:T(8,128)(2,1)} %param.7), channel_id=1, replica_groups=mesh['row'=8,'col'=4] {'col'}, dimensions={0} | all-to-all | bytes 2097152 | tf_op jit(solution)/shard_map/all_to_all | solution.py:67
  32.9 1.3 copy-done.2
  34.4 1.7 copy-done.6
  36.1 3.7 %fusion.31 = bf16[64,8,24,128]{3,1,2,0:T(8,128)(2,1)S(1)} fusion(bf16[512,1024]{1,0:T(8,128)(2,1)S(1)} %fusion.18, bf16[1024,3072]{1,0:T(8,128)(2,1)S(1)} %copy-done.6), kind=kOutput, calls=%fused_computation.46 | convolution fusion | flops 3222798336 | bytes 10485760 | tf_op jit(solution)/shard_map/dot_general | solution.py:16
  40.7 2.2 %fusion.62 = (bf16[8,64,1,8,128]{4,3,2,1,0:T(8,128)(2,1)S(1)}, bf16[8,64,1,8,128]{4,3,2,1,0:T(8,128)(2,1)}, bf16[8,64,1,8,128]{4,3,2,1,0:T(8,128)(2,1)}) fusion(bf16[8,64,3,8,128]{4,3,2,1,0:T(8,128)(2,1)S(1)} %bitcast.105), kind=kLoop, calls=%fused_computation.79 | loop fusion | bytes 6291456 | tf_op jit(solution)/shard_map/slice | solution.py:39
  42.9 2.2 %fusion.63 = f32[8,8,64]{2,1,0:T(8,128)S(1)} fusion(bf16[8,64,1,8,128]{4,3,2,1,0:T(8,128)(2,1)} %get-tuple-element.10, bf16[8,64,1,8,128]{4,3,2,1,0:T(8,128)(2,1)S(1)} %get-tuple-element.8), kind=kOutput, calls=%fused_computation.80 | convolution fusion | flops 67895360 | bytes 2113536 | tf_op jit(solution)/shard_map/sub | solution.py:23
  45.1 3.2 %fusion.43 = f32[8,8,64,64]{2,3,1,0:T(8,128)} fusion(bf16[8,64,1,8,128]{4,3,2,1,0:T(8,128)(2,1)} %get-tuple-element.10, bf16[8,64,1,8,128]{4,3,2,1,0:T(8,128)(2,1)S(1)} %get-tuple-element.8), kind=kOutput, calls=%fused_computation.59 | convolution fusion | flops 67108864 | bytes 3145728 | tf_op jit(solution)/shard_map/aqhd,akhd->ahqk/dot_general | solution.py:22
  48.3 2.8 %fusion.39 = bf16[8,8,8,8,128]{4,3,2,1,0:T(8,128)(2,1)S(1)} fusion(bf16[8,64,1,8,128]{4,3,2,1,0:T(8,128)(2,1)} %get-tuple-element.9, f32[8,8,64]{2,1,0:T(8,128)S(1)} %fusion.63, f32[8,8,64,64]{2,3,1,0:T(8,128)} %fusion.43), kind=kOutput, calls=%fused_computation.52 | convolution fusion | flops 68685888 | bytes 3162112 | tf_op jit(solution)/shard_map/ahqk,akhd->aqhd/dot_general | solution.py:24
  51.1 3.5 %fusion.19 = bf16[8,64,1024]{2,1,0:T(8,128)(2,1)S(1)} fusion(f32[4,8,16,1024]{3,2,0,1:T(8,128)} %copy-done.2, bf16[1024,1024]{1,0:T(8,128)(2,1)} %param.9, bf16[8,8,8,8,128]{4,3,2,1,0:T(8,128)(2,1)S(1)} %fusion.39), kind=kOutput, calls=%fused_computation.27 | convolution fusion | flops 1074790400 | bytes 6291456 | tf_op jit(solution)/shard_map/dot_general | solution.py:48
  55.2 28.4 %all_to_all.55 = bf16[8,64,1024]{2,0,1:T(8,128)(2,1)S(1)} all-to-all(bf16[8,64,1024]{2,0,1:T(8,128)(2,1)S(1)} %copy.87), channel_id=1, replica_groups=mesh['row'=8,'col'=4] {'row','col'}, dimensions={1} | all-to-all | bytes 2097152 | tf_op jit(solution)/shard_map/all_to_all | solution.py:71
  84.5 2.4 %copy.149 = f32[8,32,2,1024]{3,2,0,1:T(2,128)} copy(bf16[8,32,2,1024]{3,0,2,1:T(8,128)(2,1)S(1)} %bitcast.107) | data formatting | bytes 3145728 | tf_op jit(solution)/shard_map/convert_element_type | solution.py:51
  86.9 3.7 %reshape.105 = f32[512,1024]{1,0:T(8,128)} reshape(f32[32,8,2,1024]{3,2,1,0:T(2,128)} %bitcast.109) | data formatting | bytes 4194304 | tf_op jit(solution)/shard_map/convert_element_type | solution.py:51
  90.6 6.9 %fusion.32 = bf16[64,8,24,128]{3,1,2,0:T(8,128)(2,1)S(1)} fusion(bf16[1024,3072]{1,0:T(8,128)(2,1)} %param.10, f32[512,1024]{1,0:T(8,128)} %reshape.105, f32[512]{0:T(512)S(1)} %rsqrt.33), kind=kOutput, calls=%fused_computation.47 | convolution fusion | flops 3223846912 | bytes 11536384 | tf_op jit(solution)/shard_map/dot_general | solution.py:16
  98.3 1.9 fusion.61
  100.2 1.6 copy.113
  101.8 2.3 %fusion.42 = f32[2,8,256,256]{2,3,1,0:T(8,128)S(1)} fusion(bf16[256,2,1,8,128]{4,3,2,1,0:T(8,128)(2,1)} %get-tuple-element.6, bf16[256,2,1,8,128]{4,3,2,1,0:T(8,128)(2,1)} %get-tuple-element.7), kind=kOutput, calls=%fused_computation.56 | convolution fusion | flops 268435456 | bytes 6291456 | tf_op jit(solution)/shard_map/qbhd,kbhd->bhqk/dot_general | solution.py:31
  104.0 3.2 %fusion.64 = (f32[2,8,256]{2,1,0:T(8,128)S(1)}, f32[2,8,256,256]{2,3,1,0:T(8,128)S(1)}) fusion(f32[2,8,256,256]{2,3,1,0:T(8,128)S(1)} %fusion.42), kind=kOutput, calls=%fused_computation.81 | output fusion | flops 4194559 | bytes 8404992 | tf_op jit(solution)/shard_map/sub | solution.py:32
  108.9 1.7 fusion.13
  114.2 9.7 %fusion.16 = f32[512,1024]{1,0:T(8,128)} fusion(bf16[2048,1024]{1,0:T(8,128)(2,1)} %param.13, bf16[512,1024]{1,0:T(8,128)(2,1)} %reshape.98, bf16[1024,2048]{1,0:T(8,128)(2,1)} %param.12), kind=kOutput, calls=%fused_computation.23 | convolution fusion | flops 4304404480 | bytes 11534336 | tf_op jit(solution)/shard_map/dot_general | solution.py:60
  123.9 3.5 %reshape.99 = f32[256,2,1024]{2,1,0:T(2,128)} reshape(f32[512,1024]{1,0:T(8,128)} %fusion.16) | data formatting | bytes 4194304 | tf_op jit(solution)/shard_map/reshape | solution.py:60
  127.4 2.3 %fusion.15 = bf16[256,2,1024]{2,0,1:T(8,128)(2,1)S(1)} fusion(bf16[256,2,1024]{2,0,1:T(8,128)(2,1)S(1)} %copy-done.4, f32[256,2,1024]{2,1,0:T(2,128)} %reshape.99), kind=kLoop, calls=%fused_computation.22 | loop fusion | flops 1572864 | bytes 4194304 | tf_op jit(solution)/shard_map/convert_element_type | solution.py:63
  130.8 29.3 %all_to_all.56 = bf16[256,2,1024]{2,1,0:T(2,128)(2,1)S(1)} all-to-all(bf16[256,2,1024]{2,1,0:T(2,128)(2,1)S(1)} %copy.100), channel_id=1, replica_groups=mesh['row'=8,'col'=4] {'row','col'}, dimensions={0} | all-to-all | bytes 2097152 | tf_op jit(solution)/shard_map/all_to_all | solution.py:76
  160.4 30.2 %all_to_all.57 = bf16[8,64,1024]{2,0,1:T(8,128)(2,1)S(1)} all-to-all(bf16[8,64,1024]{2,0,1:T(8,128)(2,1)S(1)} %bitcast.112), channel_id=1, replica_groups=mesh['row'=8,'col'=4] {'col'}, dimensions={1} | all-to-all | bytes 2097152 | tf_op jit(solution)/shard_map/all_to_all | solution.py:77
  190.7 1.6 copy.104
  (35 shorter events, 10.5 us)
Async XLA Ops:
  0.0 107.8 %copy-start = (bf16[1024,1024]{1,0:T(8,128)(2,1)S(1)}, bf16[1024,1024]{1,0:T(8,128)(2,1)}, u32[]{:S(2)}) copy-start(bf16[1024,1024]{1,0:T(8,128)(2,1)} %param.11) | copy-start | bytes 6291460
  32.6 3.5 %copy-start.6 = (bf16[1024,3072]{1,0:T(8,128)(2,1)S(1)}, bf16[1024,3072]{1,0:T(8,128)(2,1)}, u32[]{:S(2)}) copy-start(bf16[1024,3072]{1,0:T(8,128)(2,1)} %param.8) | copy-start | bytes 18874372
  32.9 1.4 copy-start.2
  104.0 3.3 %copy-start.5 = (bf16[256,2,1,8,128]{0,4,3,1,2:T(8,128)(2,1)S(1)}, bf16[256,2,1,8,128]{0,4,3,1,2:T(8,128)(2,1)}, u32[]{:S(2)}) copy-start(bf16[256,2,1,8,128]{0,4,3,1,2:T(8,128)(2,1)} %copy.113) | copy-start | bytes 3145732
  107.3 1.6 copy-start.1
  110.6 1.0 copy-start.3
  123.9 3.5 %copy-start.4 = (bf16[256,2,1024]{2,0,1:T(8,128)(2,1)S(1)}, bf16[256,2,1024]{2,0,1:T(8,128)(2,1)}, u32[]{:S(2)}) copy-start(bf16[256,2,1024]{2,0,1:T(8,128)(2,1)} %copy-done.3) | copy-start | bytes 3145732
where the time goes:
time: 193 us; the launch traced here: 192 us
  blocking collectives  120 us (62%)
  matrix products  36.4 us (19%)
  local copies, waits for them, and re-layouts  28.9 us (15%)
  other arithmetic  6.52 us (3%)
    all_to_all x1, blocking collectives, on_device(): lax.all_to_all(latents, 'col', split_axis=0, concat_axis=1, tiled=True)  32.2 us
    all_to_all x1, blocking collectives, on_device(): lax.all_to_all(back_rows, 'col', split_axis=1, concat_axis=0, tiled=True)  30.2 us
    all_to_all x1, blocking collectives, on_device(): lax.all_to_all(output, ('row', 'col'), split_axis=0, concat_axis=1, tiled...  29.3 us
    all_to_all x1, blocking collectives, on_device(): lax.all_to_all(after1, ('row', 'col'), split_axis=1, concat_axis=0, tiled...  28.4 us
    dot_general x2, matrix products, project(): jnp.dot(normed.reshape(rows * cols, width), weight, preferred_element_typ...  10.5 us
    dot_general x1, matrix products, feed_forward(): jnp.dot(hidden, down_weight, preferred_element_type=jnp.float32)  9.68 us
    unnamed x18, local copies, waits for them, and re-layouts  8.5 us
    convert_element_type x4, local copies, waits for them, and re-layouts, add_projected(): return (base.astype(jnp.float32) + term).astype(jnp.bfloat16)  6.92 us

commit v1 on v0

v1 whole, which is shorter than its diff:
```python
import functools
import math

import jax
import jax.numpy as jnp
from jax import lax
from jax.experimental import pallas as pl
from jax.experimental.pallas import tpu as pltpu
from jax.sharding import PartitionSpec as P


HEADS = 8
CHUNKS = 2
BF = jnp.bfloat16
F32 = jnp.float32


def normalize(wide):
    return (wide * lax.rsqrt(jnp.mean(wide * wide, -1, keepdims=True) + 1e-06)).astype(BF)


def dot(a, b):
    return jnp.dot(a, b, preferred_element_type=F32)


def dot_t(a, b):
    return lax.dot_general(a, b, (((1,), (1,)), ((), ())), preferred_element_type=F32)


def attend(units, mask):
    scores = [dot_t(q, k) for q, k, _ in units]
    weights = []
    for s, (q, _, _) in zip(scores, units):
        gain = math.log2(math.e) / math.sqrt(q.shape[-1])
        if mask is not None:
            s = jnp.where(mask, s, -1e30)
        weights.append(jnp.exp2((s - jnp.max(s, -1, keepdims=True)) * gain).astype(BF))
    outs = []
    for e, (_, _, v) in zip(weights, units):
        both = dot(e, jnp.concatenate([v, jnp.ones_like(v)], -1))
        width = v.shape[-1]
        outs.append((both[:, :width] / both[:, width:]).astype(BF))
    return outs


def one_hot(source, size):
    return (lax.broadcasted_iota(jnp.int32, (source.shape[0], size), 1) == source).astype(BF)


def row_kernel(g, *refs):
    nc, nr, rows, cols, cpd = g["nc"], g["nr"], g["rows"], g["cols"], g["cpd"]
    xs, qkv, wo, outs, mixed = refs[:nc], refs[nc], refs[nc + 1], refs[nc + 2 : -1], refs[-1]
    tokens, line = rows * nc * cols, nc * cols

    def load():
        parts = [xs[k][i * cols : (i + 1) * cols, :] for i in range(rows) for k in range(nc)]
        return jnp.concatenate(parts, 0).astype(F32)

    n = normalize(load())
    group = min(max(line, 128), tokens)
    mask = None
    if group > line:
        a = lax.broadcasted_iota(jnp.int32, (group, group), 0) // line
        b = lax.broadcasted_iota(jnp.int32, (group, group), 1) // line
        mask = a == b
    width = n.shape[-1]
    head = width // HEADS
    full = dot(n, qkv[...]).astype(BF)
    where = [(slice(t, t + group), h) for h in range(HEADS) for t in range(0, tokens, group)]
    units = [[full[span, j * width + h * head : j * width + (h + 1) * head] for j in range(3)] for span, h in where]
    for (span, h), out in zip(where, attend(units, mask)):
        mixed[span, h * head : (h + 1) * head] = out
    after = (load() + dot(mixed[...], wo[...])).astype(BF)
    o = lax.broadcasted_iota(jnp.int32, (tokens, 1), 0)
    i, jj, rest = o % rows, (o // rows) % cpd, o // (rows * cpd)
    chips = nr // 2
    if len(outs) == nc:
        k, b, q = rest // nr, (rest // chips) % 2, rest % chips
    else:
        k, b, q = rest % nc, rest // (nc * chips), (rest // nc) % chips
    m = 2 * q + b
    source = (i * nc + k) * cols + cpd * jnp.bitwise_xor(m, lax.axis_index("row")) + jj
    moved = dot(one_hot(source, tokens), after).astype(BF)
    each = tokens // len(outs)
    for part, out in enumerate(outs):
        out[...] = moved[part * each : (part + 1) * each, :]


def near(x):
    return pltpu.with_memory_space_constraint(x, pltpu.VMEM)


SMEM_SPEC = pl.BlockSpec(memory_space=pltpu.SMEM)
VMEM_SPEC = pl.BlockSpec(memory_space=pltpu.VMEM)


def call(kernel, ins, outs, scratch, flops, limit=16 << 20):
    moved = sum(a.size * 2 for a in ins) + sum(math.prod(o) * 2 for o in outs)
    small = [a.dtype == jnp.int32 for a in ins]
    return pl.pallas_call(
        kernel,
        in_specs=[SMEM_SPEC if i else VMEM_SPEC for i in small],
        out_specs=[VMEM_SPEC] * len(outs),
        out_shape=[jax.ShapeDtypeStruct(o, BF) for o in outs],
        scratch_shapes=scratch,
        compiler_params=pltpu.CompilerParams(vmem_limit_bytes=limit),
        cost_estimate=pl.CostEstimate(flops=flops, bytes_accessed=moved, transcendentals=0),
    )(*[a if i else near(a) for a, i in zip(ins, small)])


def split_kernel(count, band, offset, latents, *refs):
    outs, sems = refs[:count], refs[count]
    rows = outs[0].shape[0]
    copies = []
    for k in [*range(1, count), 0]:
        at = jnp.bitwise_xor(lax.axis_index("col"), k) * band + offset
        copies.append(pltpu.make_async_copy(latents.at[pl.ds(at, rows)], outs[k], sems.at[k]))
    for copy in copies:
        copy.start()
    for copy in copies:
        copy.wait()


def split(latents, count, band, offset, rows):
    _, cols, width = latents.shape
    return pl.pallas_call(
        functools.partial(split_kernel, count, band, offset),
        in_specs=[pl.BlockSpec(memory_space=pltpu.HBM)],
        out_specs=[VMEM_SPEC] * count,
        out_shape=[pltpu.VMEM((rows, cols, width), BF)] * count,
        scratch_shapes=[pltpu.SemaphoreType.DMA((count,))],
        compiler_params=pltpu.CompilerParams(vmem_limit_bytes=1 << 20),
        cost_estimate=pl.CostEstimate(flops=0, bytes_accessed=4 * count * rows * cols * width, transcendentals=0),
        name="split",
    )(pltpu.with_memory_space_constraint(latents, pltpu.HBM))


def fetch_kernel(count, pieces, *refs):
    ins, outs, sems = refs[:count], refs[count : 2 * count], refs[2 * count]
    copies = []
    for i in range(count):
        size = ins[i].shape[0] // pieces
        for j in range(pieces):
            span = pl.ds(j * size, size)
            copies.append(pltpu.make_async_copy(ins[i].at[span], outs[i].at[span], sems.at[i, j]))
    for copy in copies:
        copy.start()
    for copy in copies:
        copy.wait()


def fetch(weights, pieces=4):
    count = len(weights)
    total = sum(2 * w.size for w in weights)
    return pl.pallas_call(
        functools.partial(fetch_kernel, count, pieces),
        in_specs=[pl.BlockSpec(memory_space=pltpu.HBM)] * count,
        out_specs=[VMEM_SPEC] * count,
        out_shape=[pltpu.VMEM(w.shape, w.dtype) for w in weights],
        scratch_shapes=[pltpu.SemaphoreType.DMA((count, pieces))],
        compiler_params=pltpu.CompilerParams(vmem_limit_bytes=1 << 20),
        cost_estimate=pl.CostEstimate(flops=0, bytes_accessed=2 * total, transcendentals=0),
        name="fetch",
    )(*[pltpu.with_memory_space_constraint(w, pltpu.HBM) for w in weights])


def row_stage(g, parts, slots, row_qkv, row_out):
    tokens = g["rows"] * g["nc"] * g["cols"]
    width = row_out.shape[0]
    return call(
        functools.partial(row_kernel, g),
        [*slots, row_qkv, row_out],
        [(tokens // parts, width)] * parts,
        [pltpu.VMEM((tokens, width), BF)],
        8 * tokens * width * width,
    )


def gather_columns(g, xs, by_row):
    cpd, rows, nr, nc = g["cpd"], g["rows"], g["nr"], g["nc"]
    x = jnp.concatenate([ref[...] for ref in xs], 0)
    tokens = x.shape[0]
    o = lax.broadcasted_iota(jnp.int32, (tokens, 1), 0)
    per = tokens // cpd
    jj, mk, i = o // per, (o % per) // rows, o % rows
    if not by_row:
        mk = (mk % nc) * nr + mk // nc
    return dot(one_hot((mk * cpd + jj) * rows + i, tokens), x)


def project_kernel(g, by_row, *refs):
    xs, w, outs, x_out = refs[:-5], refs[-5], refs[-4:-1], refs[-1]
    x = gather_columns(g, xs, by_row)
    x_out[...] = x.astype(BF)
    n = normalize(x)
    width = n.shape[-1]
    for j, out in enumerate(outs):
        out[...] = dot(n, w[:, j * width : (j + 1) * width]).astype(BF)


def project_stage(g, slots, col_qkv, by_row):
    width = col_qkv.shape[0]
    tokens = sum(a.shape[0] for a in slots)
    return call(
        functools.partial(project_kernel, g, by_row),
        [*slots, col_qkv],
        [(tokens, width)] * 4,
        [],
        6 * tokens * width * width,
    )


def group_kernel(g, members, *refs):
    nr, cpd, nc, rows = g["nr"], g["cpd"], g["nc"], g["rows"]
    old, (wo, up, down) = refs[: 4 * CHUNKS], refs[4 * CHUNKS : 4 * CHUNKS + 3]
    count = len(members)
    outs, (mixed, hidden) = refs[4 * CHUNKS + 3 :][:count], refs[4 * CHUNKS + 3 + count :]
    per = old[0].shape[0] // cpd
    each = per // nr
    width = wo.shape[0]
    head = width // HEADS

    def queries(which, lanes, jj):
        parts = []
        for t in range(CHUNKS):
            for m in members:
                at = jj * per + m * each
                parts.append(old[4 * t + which][at : at + each, lanes])
        return jnp.concatenate(parts, 0)

    def keys(which, lanes, jj):
        return jnp.concatenate([old[4 * t + which][jj * per : (jj + 1) * per, lanes] for t in range(CHUNKS)], 0)

    where = [(jj, slice(h * head, (h + 1) * head)) for h in range(HEADS) for jj in range(cpd)]
    units = [(queries(0, lanes, jj), keys(1, lanes, jj), keys(2, lanes, jj)) for jj, lanes in where]
    size = CHUNKS * count * each
    for (jj, lanes), out in zip(where, attend(units, None)):
        mixed[jj * size : (jj + 1) * size, lanes] = out
    base = jnp.concatenate([queries(3, slice(0, width), jj) for jj in range(cpd)], 0)
    after = (base.astype(F32) + dot(mixed[...], wo[...])).astype(BF)
    n = normalize(after.astype(F32))
    block = min(512, up.shape[1])
    for b in range(0, up.shape[1], block):
        hidden[:, b : b + block] = jax.nn.gelu(dot(n, up[:, b : b + block]), approximate=True).astype(BF)
    result = (after.astype(F32) + dot(hidden[...], down[...])).astype(BF)
    tokens = result.shape[0]
    o = lax.broadcasted_iota(jnp.int32, (tokens, 1), 0)
    jj, i, t = o % cpd, (o // cpd) % rows, (o // (cpd * rows)) % CHUNKS
    c, m = (o // (cpd * rows * CHUNKS)) % nc, o // (cpd * rows * CHUNKS * nc)
    k = jnp.bitwise_xor(c, lax.axis_index("col"))
    source = (((jj * CHUNKS + t) * count + m) * nc + k) * rows + i
    moved = dot(one_hot(source, tokens), result).astype(BF)
    size = tokens // count
    for m in range(count):
        outs[m][...] = moved[m * size : (m + 1) * size, :]


def group_stage(g, members, old, col_out, up_weight, down_weight):
    width, hidden = up_weight.shape
    count = len(members)
    size = CHUNKS * old[0].shape[0] // g["nr"]
    tokens = count * size
    return call(
        functools.partial(group_kernel, g, members),
        [*old, col_out, up_weight, down_weight],
        [(size, width)] * count,
        [pltpu.VMEM((tokens, width), BF), pltpu.VMEM((tokens, hidden), BF)],
        4 * tokens * width * hidden,
    )


def final_kernel(g, *refs):
    nr, cpd, cols, span = g["nr"], g["cpd"], g["cols"], g["span"]
    ins, out = refs[:nr], refs[nr]
    tokens = span * cols
    o = lax.broadcasted_iota(jnp.int32, (tokens, 1), 0)
    w, j = o // cols, o % cols
    m = jnp.bitwise_xor(j // cpd, lax.axis_index("row"))
    pick = one_hot((m * span + w) * cpd + j % cpd, tokens)
    rows = ins[0].shape[0] // cpd
    for a in range(0, rows, span):
        x = jnp.concatenate([ref[a * cpd : (a + span) * cpd, :] for ref in ins], 0)
        out[a * cols : (a + span) * cols, :] = dot(pick, x).astype(BF)


def final_stage(g, slots):
    each, width = slots[0].shape
    total = g["nr"] * each
    (out,) = call(
        functools.partial(final_kernel, g), [*slots], [(total, width)], [], 2 * total * width * g["span"] * g["cols"]
    )
    return out


def swap(x, axis, size, k):
    return x if k == 0 else lax.ppermute(x, axis, [(i, i ^ k) for i in range(size)])


def exchange(parts, axis, order, shift=0):
    n = len(parts)
    size = n << shift
    got = {0: parts[0]}
    for k in order:
        got[k] = swap(parts[k], axis, size, k << shift)
    return [got[k] for k in range(n)]


def deal_kernel(plan, *refs):
    ins, outs = refs[: -len(plan)], refs[-len(plan) :]
    for out, pieces in zip(outs, plan):
        at = 0
        for i, start, size in pieces:
            out[at : at + size, :] = ins[i][start : start + size, :]
            at += size


def deal(ins, plan):
    width = ins[0].shape[1]
    return call(functools.partial(deal_kernel, plan), ins, [(sum(p[2] for p in pieces), width) for pieces in plan], [], 0)


def row_hop(ins, own, sent, cells, nr):
    came = swap(sent, "row", nr, 1)
    chips = nr // 2
    count = len(ins)
    plan = [own(q) + [(count, start, size) for start, size in cells(q)] for q in range(chips)]
    parts = deal([*ins, came], plan)
    return spread(parts, chip_order(nr))


def spread(parts, order):
    n = len(parts)
    got = {0: parts[0]}
    for q in order:
        got[q] = lax.ppermute(parts[q], "row", [(i, i ^ (2 * q)) for i in range(2 * n)])
    return [got[q] for q in range(n)]


def on_device(nr, nc, latents, row_qkv, row_out, col_qkv, col_out, up_weight, down_weight):
    local_rows, cols, width = latents.shape
    band = local_rows // nc
    rows = band // CHUNKS
    cpd = cols // nr
    chips = nr // 2
    cell = rows * cpd
    g = dict(nr=nr, nc=nc, rows=rows, cols=cols, cpd=cpd, span=8)
    z_order = list(range(nc - 1, 0, -1))

    def enter(t, latents):
        slots = split(latents, nc, band, t * rows, rows)
        slots = [a.reshape(rows * cols, width) for a in slots]
        return exchange(slots, "col", z_order)

    first = enter(0, latents)
    weights = fetch([row_qkv, row_out, col_qkv, col_out])
    latents, row_qkv, row_out, col_qkv, col_out = lax.optimization_barrier((latents, *weights))
    second = enter(1, latents)

    parts = row_stage(g, nc, first, row_qkv, row_out)
    up_weight, down_weight = fetch([up_weight, down_weight])
    parts = exchange(parts, "col", z_order)
    half = chips * cell
    (sent,) = deal(parts, [[(k, half, half) for k in range(nc)]])
    slots0 = row_hop(
        parts,
        lambda q: [(k, q * cell, cell) for k in range(nc)],
        sent,
        lambda q: [(k * half + q * cell, cell) for k in range(nc)],
        nr,
    )

    stay, sent = row_stage(g, 2, second, row_qkv, row_out)
    size = nc * cell
    parts = row_hop([stay], lambda q: [(0, q * size, size)], sent, lambda q: [(q * size, size)], nr)
    plan = [[(q, b * size + k * cell, cell) for q in range(chips) for b in range(2)] for k in range(nc)]
    parts = deal(parts, plan)
    slots1 = exchange(parts, "col", z_order)

    old = project_stage(g, slots0, col_qkv, True)
    old += project_stage(g, slots1, col_qkv, False)
    final = [None] * nr
    for members in groups(nr):
        outs = group_stage(g, members, old, col_out, up_weight, down_weight)
        for m, out in zip(members, outs):
            final[m] = swap(out, "row", nr, m)
    return final_stage(g, final).reshape(local_rows, cols, width)


def chip_order(nr):
    return sorted(range(1, nr // 2), key=lambda q: bin(q).count("1"))


def groups(nr):
    near = sorted([*range(2, nr, 2), nr - 1], key=lambda m: bin(m // 2).count("1"))
    return near, [m for m in range(nr - 1, -1, -1) if m not in near]


def solution(mesh):
    in_specs = (P("row", "col", None), P(), P(), P(), P(), P(), P())
    return jax.shard_map(
        functools.partial(on_device, mesh.shape["row"], mesh.shape["col"]),
        mesh=mesh,
        in_specs=in_specs,
        out_specs=P("row", "col", None),
        check_vma=False,
    )
```

time: 193 us -> 103 us (0.53)
  blocking collectives: 120 us -> 0 us
  matrix products: 36.4 us -> 0 us
  waiting for transfers between devices: 0 us -> 35.8 us
  starting transfers between devices: 0 us -> 34.2 us
  Pallas kernels: 0 us -> 32.8 us
  local copies, waits for them, and re-layouts: 28.9 us -> 0 us
  other arithmetic: 6.52 us -> 0 us
    all_to_all x4 -> x0, blocking collectives: 120 us -> none  [the longest x1 32.2 us: on_device(): lax.all_to_all(latents, 'col', split_axis=0, concat_axis=1, tiled=True)]
    ppermute x0 -> x27, waiting for transfers between devices: none -> 35.8 us  [the longest x21 29.4 us: swap(): lax.ppermute(x, axis, [(i, i ^ k) for i in range(size)])]
    ppermute x0 -> x27, starting transfers between devices: none -> 34.2 us  [the longest x21 27.1 us: swap(): lax.ppermute(x, axis, [(i, i ^ k) for i in range(size)])]
    dot_general x9 -> x0, matrix products: 34.2 us -> none  [the longest x2 10.5 us: project(): jnp.dot(normed.reshape(rows * cols, width), weight, preferred_element_typ...]
    pallas_call x0 -> x15, Pallas kernels: none -> 32.8 us  [the longest x11 21.2 us: call(): pl.pallas_call(kernel, in_specs=[SMEM_SPEC if i else VMEM_SPEC for i in s...]
    convert_element_type x6 -> x0, local copies, waits for them, and re-layouts: 9.08 us -> none  [the longest x4 6.92 us: add_projected(): return (base.astype(jnp.float32) + term).astype(jnp.bfloat16)]
    unnamed x18 -> x0, local copies, waits for them, and re-layouts: 8.5 us -> none
    reshape x2 -> x0, local copies, waits for them, and re-layouts: 4.79 us -> none  [the longest x1 3.54 us: feed_forward(): jnp.dot(hidden, down_weight, preferred_element_type=jnp.float32)]
  transfers between devices with their start and end apart: 0 -> 27, of which waited for: 0 -> 9; matrix products, arithmetic and copies ran while one was open for 0% -> 0% of each run, Pallas kernels for 0% -> 17%
where the time goes in v1:
time: 103 us
  waiting for transfers between devices  35.8 us (35%)
  starting transfers between devices  34.2 us (33%)
  Pallas kernels  32.8 us (32%)
    ppermute x21, waiting for transfers between devices, swap(): lax.ppermute(x, axis, [(i, i ^ k) for i in range(size)])  29.4 us
    ppermute x21, starting transfers between devices, swap(): lax.ppermute(x, axis, [(i, i ^ k) for i in range(size)])  27.1 us
    pallas_call x11, Pallas kernels, call(): pl.pallas_call(kernel, in_specs=[SMEM_SPEC if i else VMEM_SPEC for i in s...  21.2 us
    pallas_call x2, Pallas kernels, fetch(): pl.pallas_call(functools.partial(fetch_kernel, count, pieces), in_specs=[...  9.36 us
    ppermute x6, starting transfers between devices, spread(): lax.ppermute(parts[q], 'row', [(i, i ^ 2 * q) for i in range(2 * n)])  7.11 us
    ppermute x6, waiting for transfers between devices, spread(): lax.ppermute(parts[q], 'row', [(i, i ^ 2 * q) for i in range(2 * n)])  6.43 us
    pallas_call x2, Pallas kernels, split(): pl.pallas_call(functools.partial(split_kernel, count, band, offset), in_s...  2.26 us
  transfers between devices with their start and end apart: 27, of which 9 were waited for; matrix products, arithmetic and copies ran while one was open for 0% of the time, Pallas kernels for 17%

profile of v1, /device:TPU:0, one launch (start us, length us, event | category | flops | bytes accessed | tf_op | source)
XLA Modules:
  0.0 103.1 jit_solution(9042249335916633034)
XLA Ops:
  0.0 5.9 %fetch.2 = (bf16[1024,3072]{1,0:T(8,128)(2,1)S(1)}, bf16[1024,1024]{1,0:T(8,128)(2,1)S(1)}, bf16[1024,3072]{1,0:T(8,128)(2,1)S(1)}, bf16[1024,1024]{1,0:T(8,128)(2,1)S(1)}) custom-call(bf16[1024,3072]{1,0:T(8,128)(2,1)} %refs_0_.2, bf16[1024,1024]{1,0:T(8,128)(2,1)} %refs_1_.2, bf16[1024,3072]{1,0:T(8,128)(2,1)} %refs_2_.1, bf16[1024,1024]{1,0:T(8,128)(2,1)} %refs_3_.1), custom_call_target="tpu_custom_call" | custom-call | bytes 33554432 | tf_op jit(solution)/shard_map/fetch/pallas_call | solution.py:155
  7.0 3.1 %collective-permute-start.10 = (bf16[64,1024]{1,0:T(8,128)(2,1)S(1)}, bf16[64,1024]{1,0:T(8,128)(2,1)S(1)}, u32[]{:S(2)}, u32[]{:S(2)}) collective-permute-start(bf16[64,1024]{1,0:T(8,128)(2,1)S(1)} %bitcast.16), channel_id=1, source_target_pairs={{0,1},{1,0},{2,3},{3,2},{4,5},{5,4},{6,7},{7,6},{8,9},{9,8},{10,11... | collective-permute-start | bytes 393224 | tf_op jit(solution)/shard_map/ppermute | solution.py:296
  10.2 2.6 %collective-permute-start.11 = (bf16[64,1024]{1,0:T(8,128)(2,1)S(1)}, bf16[64,1024]{1,0:T(8,128)(2,1)S(1)}, u32[]{:S(2)}, u32[]{:S(2)}) collective-permute-start(bf16[64,1024]{1,0:T(8,128)(2,1)S(1)} %bitcast.15), channel_id=1, source_target_pairs={{0,2},{1,3},{2,0},{3,1},{4,6},{5,7},{6,4},{7,5},{8,10},{9,11},{10,... | collective-permute-start | bytes 393224 | tf_op jit(solution)/shard_map/ppermute | solution.py:296
  14.8 3.5 %collective-permute-start.1 = (bf16[64,1024]{1,0:T(8,128)(2,1)S(1)}, bf16[64,1024]{1,0:T(8,128)(2,1)S(1)}, u32[]{:S(2)}, u32[]{:S(2)}) collective-permute-start(bf16[64,1024]{1,0:T(8,128)(2,1)S(1)} %bitcast.12), channel_id=1, source_target_pairs={{0,2},{1,3},{2,0},{3,1},{4,6},{5,7},{6,4},{7,5},{8,10},{9,11},{10,... | collective-permute-start | bytes 393224 | tf_op jit(solution)/shard_map/ppermute | solution.py:296
  19.0 4.1 %collective-permute-done.11.refs_2_ = bf16[64,1024]{1,0:T(8,128)(2,1)S(1)} collective-permute-done((bf16[64,1024]{1,0:T(8,128)(2,1)S(1)}, bf16[64,1024]{1,0:T(8,128)(2,1)S(1)}, u32[]{:S(2)}, u32[]{:S(2)}) %collective-permute-start.11) | collective-permute-done | bytes 131104 | tf_op jit(solution)/shard_map/ppermute | solution.py:296
  23.1 3.3 %shard_map.77 = (bf16[128,1024]{1,0:T(8,128)(2,1)S(1)}, bf16[128,1024]{1,0:T(8,128)(2,1)S(1)}) custom-call(bf16[64,1024]{1,0:T(8,128)(2,1)S(1)} %bitcast.10, bf16[64,1024]{1,0:T(8,128)(2,1)S(1)} %collective-permute-done.10.refs_1_, bf16[64,1024]{1,0:T(8,128)(2,1)S(1)} %collective-permute-done.11.refs_2_, ...), custom_call_target="tpu_custom_call" | custom-call | flops 2147483648 | bytes 9437184 | tf_op jit(solution)/shard_map/pallas_call | solution.py:100
  26.5 7.8 %collective-permute-done.1.refs_2_ = bf16[64,1024]{1,0:T(8,128)(2,1)S(1)} collective-permute-done((bf16[64,1024]{1,0:T(8,128)(2,1)S(1)}, bf16[64,1024]{1,0:T(8,128)(2,1)S(1)}, u32[]{:S(2)}, u32[]{:S(2)}) %collective-permute-start.1) | collective-permute-done | bytes 131104 | tf_op jit(solution)/shard_map/ppermute | solution.py:296
  34.3 3.3 %shard_map.73 = (bf16[64,1024]{1,0:T(8,128)(2,1)S(1)}, bf16[64,1024]{1,0:T(8,128)(2,1)S(1)}, bf16[64,1024]{1,0:T(8,128)(2,1)S(1)}, bf16[64,1024]{1,0:T(8,128)(2,1)S(1)}) custom-call(bf16[64,1024]{1,0:T(8,128)(2,1)S(1)} %bitcast.9, bf16[64,1024]{1,0:T(8,128)(2,1)S(1)} %collective-permute-done.refs_1_, bf16[64,1024]{1,0:T(8,128)(2,1)S(1)} %collective-permute-done.1.refs_2_, ...), custom_call_target="tpu_custom_call" | custom-call | flops 2147483648 | bytes 9437184 | tf_op jit(solution)/shard_map/pallas_call | solution.py:100
  37.6 2.1 %collective-permute-start.3 = (bf16[64,1024]{1,0:T(8,128)(2,1)S(1)}, bf16[64,1024]{1,0:T(8,128)(2,1)S(1)}, u32[]{:S(2)}, u32[]{:S(2)}) collective-permute-start(bf16[64,1024]{1,0:T(8,128)(2,1)S(1)} %get-tuple-element.69), channel_id=1, source_target_pairs={{0,1},{1,0},{2,3},{3,2},{4,5},{5,4},{6,7},{7,6},{8,9},{9,8},{10,11... | collective-permute-start | bytes 393224 | tf_op jit(solution)/shard_map/ppermute | solution.py:296
  42.2 2.2 %collective-permute-done.3.refs_1_ = bf16[64,1024]{1,0:T(8,128)(2,1)S(1)} collective-permute-done((bf16[64,1024]{1,0:T(8,128)(2,1)S(1)}, bf16[64,1024]{1,0:T(8,128)(2,1)S(1)}, u32[]{:S(2)}, u32[]{:S(2)}) %collective-permute-start.3) | collective-permute-done | bytes 131104 | tf_op jit(solution)/shard_map/ppermute | solution.py:296
  44.4 7.9 %collective-permute-done.4.refs_2_ = bf16[64,1024]{1,0:T(8,128)(2,1)S(1)} collective-permute-done((bf16[64,1024]{1,0:T(8,128)(2,1)S(1)}, bf16[64,1024]{1,0:T(8,128)(2,1)S(1)}, u32[]{:S(2)}, u32[]{:S(2)}) %collective-permute-start.4) | collective-permute-done | bytes 131104 | tf_op jit(solution)/shard_map/ppermute | solution.py:296
  52.5 1.6 %collective-permute-start.14 = (bf16[64,1024]{1,0:T(8,128)(2,1)S(1)}, bf16[64,1024]{1,0:T(8,128)(2,1)S(1)}, u32[]{:S(2)}, u32[]{:S(2)}) collective-permute-start(bf16[64,1024]{1,0:T(8,128)(2,1)S(1)} %get-tuple-element.89), channel_id=1, source_target_pairs={{0,8},{4,12},{8,0},{12,4},{16,24},{20,28},{24,16},{28,20},{1,9},{5... | collective-permute-start | bytes 393224 | tf_op jit(solution)/shard_map/ppermute | solution.py:335
  56.0 2.8 %collective-permute-done.14.refs_1_ = bf16[64,1024]{1,0:T(8,128)(2,1)S(1)} collective-permute-done((bf16[64,1024]{1,0:T(8,128)(2,1)S(1)}, bf16[64,1024]{1,0:T(8,128)(2,1)S(1)}, u32[]{:S(2)}, u32[]{:S(2)}) %collective-permute-start.14) | collective-permute-done | bytes 131104 | tf_op jit(solution)/shard_map/ppermute | solution.py:335
  58.8 3.6 %collective-permute-done.15.refs_2_ = bf16[64,1024]{1,0:T(8,128)(2,1)S(1)} collective-permute-done((bf16[64,1024]{1,0:T(8,128)(2,1)S(1)}, bf16[64,1024]{1,0:T(8,128)(2,1)S(1)}, u32[]{:S(2)}, u32[]{:S(2)}) %collective-permute-start.15) | collective-permute-done | bytes 131104 | tf_op jit(solution)/shard_map/ppermute | solution.py:335
  62.5 2.2 %collective-permute-start.17 = (bf16[64,1024]{1,0:T(8,128)(2,1)S(1)}, bf16[64,1024]{1,0:T(8,128)(2,1)S(1)}, u32[]{:S(2)}, u32[]{:S(2)}) collective-permute-start(bf16[64,1024]{1,0:T(8,128)(2,1)S(1)} %get-tuple-element.93), channel_id=1, source_target_pairs={{0,1},{1,0},{2,3},{3,2},{4,5},{5,4},{6,7},{7,6},{8,9},{9,8},{10,11... | collective-permute-start | bytes 393224 | tf_op jit(solution)/shard_map/ppermute | solution.py:296
  67.1 3.5 %fetch.3 = (bf16[1024,2048]{1,0:T(8,128)(2,1)S(1)}, bf16[2048,1024]{1,0:T(8,128)(2,1)S(1)}) custom-call(bf16[1024,2048]{1,0:T(8,128)(2,1)} %refs_0_.3, bf16[2048,1024]{1,0:T(8,128)(2,1)} %refs_1_.3), custom_call_target="tpu_custom_call" | custom-call | bytes 16777216 | tf_op jit(solution)/shard_map/fetch/pallas_call | solution.py:155
  74.2 2.7 %collective-permute-done.18.refs_2_ = bf16[64,1024]{1,0:T(8,128)(2,1)S(1)} collective-permute-done((bf16[64,1024]{1,0:T(8,128)(2,1)S(1)}, bf16[64,1024]{1,0:T(8,128)(2,1)S(1)}, u32[]{:S(2)}, u32[]{:S(2)}) %collective-permute-start.18) | collective-permute-done | bytes 131104 | tf_op jit(solution)/shard_map/ppermute | solution.py:296
  76.9 2.1 %shard_map.80 = (bf16[256,1024]{1,0:T(8,128)(2,1)S(1)}, bf16[256,1024]{1,0:T(8,128)(2,1)S(1)}, bf16[256,1024]{1,0:T(8,128)(2,1)S(1)}, bf16[256,1024]{1,0:T(8,128)(2,1)S(1)}) custom-call(bf16[64,1024]{1,0:T(8,128)(2,1)S(1)} %get-tuple-element.92.refs_0_, bf16[64,1024]{1,0:T(8,128)(2,1)S(1)} %collective-permute-done.17.refs_1_, ...), custom_call_target="tpu_custom_call" | custom-call | flops 1610612736 | bytes 8912896 | tf_op jit(solution)/shard_map/pallas_call | solution.py:100
  79.1 2.1 %shard_map.76 = (bf16[256,1024]{1,0:T(8,128)(2,1)S(1)}, bf16[256,1024]{1,0:T(8,128)(2,1)S(1)}, bf16[256,1024]{1,0:T(8,128)(2,1)S(1)}, bf16[256,1024]{1,0:T(8,128)(2,1)S(1)}) custom-call(bf16[64,1024]{1,0:T(8,128)(2,1)S(1)} %get-tuple-element.72.refs_0_, bf16[64,1024]{1,0:T(8,128)(2,1)S(1)} %collective-permute-done.7.refs_1_, ...), custom_call_target="tpu_custom_call" | custom-call | flops 1610612736 | bytes 8912896 | tf_op jit(solution)/shard_map/pallas_call | solution.py:100
  81.2 4.5 %shard_map.82 = (bf16[64,1024]{1,0:T(8,128)(2,1)S(1)}, bf16[64,1024]{1,0:T(8,128)(2,1)S(1)}, bf16[64,1024]{1,0:T(8,128)(2,1)S(1)}, bf16[64,1024]{1,0:T(8,128)(2,1)S(1)}) custom-call(bf16[256,1024]{1,0:T(8,128)(2,1)S(1)} %get-tuple-element.77.refs_0_, bf16[256,1024]{1,0:T(8,128)(2,1)S(1)} %get-tuple-element.78.refs_1_, ...), custom_call_target="tpu_custom_call" | custom-call | flops 2147483648 | bytes 15204352 | tf_op jit(solution)/shard_map/pallas_call | solution.py:100
  85.7 1.7 %collective-permute-start.21 = (bf16[64,1024]{1,0:T(8,128)(2,1)S(1)}, bf16[64,1024]{1,0:T(8,128)(2,1)S(1)}, u32[]{:S(2)}, u32[]{:S(2)}) collective-permute-start(bf16[64,1024]{1,0:T(8,128)(2,1)S(1)} %get-tuple-element.105), channel_id=1, source_target_pairs={{0,8},{4,12},{8,0},{12,4},{16,24},{20,28},{24,16},{28,20},{1,9},{5... | collective-permute-start | bytes 393224 | tf_op jit(solution)/shard_map/ppermute | solution.py:296
  89.2 4.3 %shard_map.81 = (bf16[64,1024]{1,0:T(8,128)(2,1)S(1)}, bf16[64,1024]{1,0:T(8,128)(2,1)S(1)}, bf16[64,1024]{1,0:T(8,128)(2,1)S(1)}, bf16[64,1024]{1,0:T(8,128)(2,1)S(1)}) custom-call(bf16[256,1024]{1,0:T(8,128)(2,1)S(1)} %get-tuple-element.77.refs_0_, bf16[256,1024]{1,0:T(8,128)(2,1)S(1)} %get-tuple-element.78.refs_1_, ...), custom_call_target="tpu_custom_call" | custom-call | flops 2147483648 | bytes 15204352 | tf_op jit(solution)/shard_map/pallas_call | solution.py:100
  93.5 1.8 %collective-permute-start.20 = (bf16[64,1024]{1,0:T(8,128)(2,1)S(1)}, bf16[64,1024]{1,0:T(8,128)(2,1)S(1)}, u32[]{:S(2)}, u32[]{:S(2)}) collective-permute-start(bf16[64,1024]{1,0:T(8,128)(2,1)S(1)} %get-tuple-element.104), channel_id=1, source_target_pairs={{0,4},{4,0},{8,12},{12,8},{16,20},{20,16},{24,28},{28,24},{1,5},{5... | collective-permute-start | bytes 393224 | tf_op jit(solution)/shard_map/ppermute | solution.py:296
  96.9 3.9 %collective-permute-done.22.refs_3_ = bf16[64,1024]{1,0:T(8,128)(2,1)S(1)} collective-permute-done((bf16[64,1024]{1,0:T(8,128)(2,1)S(1)}, bf16[64,1024]{1,0:T(8,128)(2,1)S(1)}, u32[]{:S(2)}, u32[]{:S(2)}) %collective-permute-start.22) | collective-permute-done | bytes 131104 | tf_op jit(solution)/shard_map/ppermute | solution.py:296
  (45 shorter events, 20.4 us)
Async XLA Ops:
  7.0 11.3 %collective-permute-start.10 = (bf16[64,1024]{1,0:T(8,128)(2,1)S(1)}, bf16[64,1024]{1,0:T(8,128)(2,1)S(1)}, u32[]{:S(2)}, u32[]{:S(2)}) collective-permute-start(bf16[64,1024]{1,0:T(8,128)(2,1)S(1)} %bitcast.16), channel_id=1, source_target_pairs={{0,1},{1,0},{2,3},{3,2},{4,5},{5,4},{6,7},{7,6},{8,9},{9,8},{10,11... | collective-permute-start | bytes 393224 | tf_op jit(solution)/shard_map/ppermute | solution.py:296
  10.2 12.9 %collective-permute-start.11 = (bf16[64,1024]{1,0:T(8,128)(2,1)S(1)}, bf16[64,1024]{1,0:T(8,128)(2,1)S(1)}, u32[]{:S(2)}, u32[]{:S(2)}) collective-permute-start(bf16[64,1024]{1,0:T(8,128)(2,1)S(1)} %bitcast.15), channel_id=1, source_target_pairs={{0,2},{1,3},{2,0},{3,1},{4,6},{5,7},{6,4},{7,5},{8,10},{9,11},{10,... | collective-permute-start | bytes 393224 | tf_op jit(solution)/shard_map/ppermute | solution.py:296
  12.7 10.3 %collective-permute-start.12 = (bf16[64,1024]{1,0:T(8,128)(2,1)S(1)}, bf16[64,1024]{1,0:T(8,128)(2,1)S(1)}, u32[]{:S(2)}, u32[]{:S(2)}) collective-permute-start(bf16[64,1024]{1,0:T(8,128)(2,1)S(1)} %bitcast.14), channel_id=1, source_target_pairs={{0,3},{1,2},{2,1},{3,0},{4,7},{5,6},{6,5},{7,4},{8,11},{9,10},{10,... | collective-permute-start | bytes 393224 | tf_op jit(solution)/shard_map/ppermute | solution.py:296
  13.9 12.6 %collective-permute-start = (bf16[64,1024]{1,0:T(8,128)(2,1)S(1)}, bf16[64,1024]{1,0:T(8,128)(2,1)S(1)}, u32[]{:S(2)}, u32[]{:S(2)}) collective-permute-start(bf16[64,1024]{1,0:T(8,128)(2,1)S(1)} %bitcast.13), channel_id=1, source_target_pairs={{0,1},{1,0},{2,3},{3,2},{4,5},{5,4},{6,7},{7,6},{8,9},{9,8},{10,11... | collective-permute-start | bytes 393224 | tf_op jit(solution)/shard_map/ppermute | solution.py:296
  14.8 19.4 %collective-permute-start.1 = (bf16[64,1024]{1,0:T(8,128)(2,1)S(1)}, bf16[64,1024]{1,0:T(8,128)(2,1)S(1)}, u32[]{:S(2)}, u32[]{:S(2)}) collective-permute-start(bf16[64,1024]{1,0:T(8,128)(2,1)S(1)} %bitcast.12), channel_id=1, source_target_pairs={{0,2},{1,3},{2,0},{3,1},{4,6},{5,7},{6,4},{7,5},{8,10},{9,11},{10,... | collective-permute-start | bytes 393224 | tf_op jit(solution)/shard_map/ppermute | solution.py:296
  18.3 15.9 %collective-permute-start.2 = (bf16[64,1024]{1,0:T(8,128)(2,1)S(1)}, bf16[64,1024]{1,0:T(8,128)(2,1)S(1)}, u32[]{:S(2)}, u32[]{:S(2)}) collective-permute-start(bf16[64,1024]{1,0:T(8,128)(2,1)S(1)} %bitcast.11), channel_id=1, source_target_pairs={{0,3},{1,2},{2,1},{3,0},{4,7},{5,6},{6,5},{7,4},{8,11},{9,10},{10,... | collective-permute-start | bytes 393224 | tf_op jit(solution)/shard_map/ppermute | solution.py:296
  26.4 26.0 %collective-permute-start.13 = (bf16[128,1024]{1,0:T(8,128)(2,1)S(1)}, bf16[128,1024]{1,0:T(8,128)(2,1)S(1)}, u32[]{:S(2)}, u32[]{:S(2)}) collective-permute-start(bf16[128,1024]{1,0:T(8,128)(2,1)S(1)} %get-tuple-element.87), channel_id=1, source_target_pairs={{0,4},{4,0},{8,12},{12,8},{16,20},{20,16},{24,28},{28,24},{1,5},{5... | collective-permute-start | bytes 786440 | tf_op jit(solution)/shard_map/ppermute | solution.py:296
  37.6 6.8 %collective-permute-start.3 = (bf16[64,1024]{1,0:T(8,128)(2,1)S(1)}, bf16[64,1024]{1,0:T(8,128)(2,1)S(1)}, u32[]{:S(2)}, u32[]{:S(2)}) collective-permute-start(bf16[64,1024]{1,0:T(8,128)(2,1)S(1)} %get-tuple-element.69), channel_id=1, source_target_pairs={{0,1},{1,0},{2,3},{3,2},{4,5},{5,4},{6,7},{7,6},{8,9},{9,8},{10,11... | collective-permute-start | bytes 393224 | tf_op jit(solution)/shard_map/ppermute | solution.py:296
  39.7 12.6 %collective-permute-start.4 = (bf16[64,1024]{1,0:T(8,128)(2,1)S(1)}, bf16[64,1024]{1,0:T(8,128)(2,1)S(1)}, u32[]{:S(2)}, u32[]{:S(2)}) collective-permute-start(bf16[64,1024]{1,0:T(8,128)(2,1)S(1)} %get-tuple-element.70), channel_id=1, source_target_pairs={{0,2},{1,3},{2,0},{3,1},{4,6},{5,7},{6,4},{7,5},{8,10},{9,11},{10,... | collective-permute-start | bytes 393224 | tf_op jit(solution)/shard_map/ppermute | solution.py:296
  40.8 11.5 %collective-permute-start.5 = (bf16[64,1024]{1,0:T(8,128)(2,1)S(1)}, bf16[64,1024]{1,0:T(8,128)(2,1)S(1)}, u32[]{:S(2)}, u32[]{:S(2)}) collective-permute-start(bf16[64,1024]{1,0:T(8,128)(2,1)S(1)} %get-tuple-element.71), channel_id=1, source_target_pairs={{0,3},{1,2},{2,1},{3,0},{4,7},{5,6},{6,5},{7,4},{8,11},{9,10},{10,... | collective-permute-start | bytes 393224 | tf_op jit(solution)/shard_map/ppermute | solution.py:296
  52.3 18.3 %collective-permute-start.6 = (bf16[128,1024]{1,0:T(8,128)(2,1)S(1)}, bf16[128,1024]{1,0:T(8,128)(2,1)S(1)}, u32[]{:S(2)}, u32[]{:S(2)}) collective-permute-start(bf16[128,1024]{1,0:T(8,128)(2,1)S(1)} %shard_map.74), channel_id=1, source_target_pairs={{0,4},{4,0},{8,12},{12,8},{16,20},{20,16},{24,28},{28,24},{1,5},{5... | collective-permute-start | bytes 786440 | tf_op jit(solution)/shard_map/ppermute | solution.py:296
  52.5 6.4 %collective-permute-start.14 = (bf16[64,1024]{1,0:T(8,128)(2,1)S(1)}, bf16[64,1024]{1,0:T(8,128)(2,1)S(1)}, u32[]{:S(2)}, u32[]{:S(2)}) collective-permute-start(bf16[64,1024]{1,0:T(8,128)(2,1)S(1)} %get-tuple-element.89), channel_id=1, source_target_pairs={{0,8},{4,12},{8,0},{12,4},{16,24},{20,28},{24,16},{28,20},{1,9},{5... | collective-permute-start | bytes 393224 | tf_op jit(solution)/shard_map/ppermute | solution.py:335
  54.0 8.4 %collective-permute-start.15 = (bf16[64,1024]{1,0:T(8,128)(2,1)S(1)}, bf16[64,1024]{1,0:T(8,128)(2,1)S(1)}, u32[]{:S(2)}, u32[]{:S(2)}) collective-permute-start(bf16[64,1024]{1,0:T(8,128)(2,1)S(1)} %get-tuple-element.90), channel_id=1, source_target_pairs={{0,16},{4,20},{8,24},{12,28},{16,0},{20,4},{24,8},{28,12},{1,17},{... | collective-permute-start | bytes 393224 | tf_op jit(solution)/shard_map/ppermute | solution.py:335
  55.6 6.9 %collective-permute-start.16 = (bf16[64,1024]{1,0:T(8,128)(2,1)S(1)}, bf16[64,1024]{1,0:T(8,128)(2,1)S(1)}, u32[]{:S(2)}, u32[]{:S(2)}) collective-permute-start(bf16[64,1024]{1,0:T(8,128)(2,1)S(1)} %get-tuple-element.91), channel_id=1, source_target_pairs={{0,24},{4,28},{8,16},{12,20},{16,8},{20,12},{24,0},{28,4},{1,25},{... | collective-permute-start | bytes 393224 | tf_op jit(solution)/shard_map/ppermute | solution.py:335
  62.5 10.3 %collective-permute-start.17 = (bf16[64,1024]{1,0:T(8,128)(2,1)S(1)}, bf16[64,1024]{1,0:T(8,128)(2,1)S(1)}, u32[]{:S(2)}, u32[]{:S(2)}) collective-permute-start(bf16[64,1024]{1,0:T(8,128)(2,1)S(1)} %get-tuple-element.93), channel_id=1, source_target_pairs={{0,1},{1,0},{2,3},{3,2},{4,5},{5,4},{6,7},{7,6},{8,9},{9,8},{10,11... | collective-permute-start | bytes 393224 | tf_op jit(solution)/shard_map/ppermute | solution.py:296
  64.7 12.2 %collective-permute-start.18 = (bf16[64,1024]{1,0:T(8,128)(2,1)S(1)}, bf16[64,1024]{1,0:T(8,128)(2,1)S(1)}, u32[]{:S(2)}, u32[]{:S(2)}) collective-permute-start(bf16[64,1024]{1,0:T(8,128)(2,1)S(1)} %get-tuple-element.94), channel_id=1, source_target_pairs={{0,2},{1,3},{2,0},{3,1},{4,6},{5,7},{6,4},{7,5},{8,10},{9,11},{10,... | collective-permute-start | bytes 393224 | tf_op jit(solution)/shard_map/ppermute | solution.py:296
  65.6 11.3 %collective-permute-start.19 = (bf16[64,1024]{1,0:T(8,128)(2,1)S(1)}, bf16[64,1024]{1,0:T(8,128)(2,1)S(1)}, u32[]{:S(2)}, u32[]{:S(2)}) collective-permute-start(bf16[64,1024]{1,0:T(8,128)(2,1)S(1)} %get-tuple-element.95), channel_id=1, source_target_pairs={{0,3},{1,2},{2,1},{3,0},{4,7},{5,6},{6,5},{7,4},{8,11},{9,10},{10,... | collective-permute-start | bytes 393224 | tf_op jit(solution)/shard_map/ppermute | solution.py:296
  70.7 8.4 %collective-permute-start.7 = (bf16[64,1024]{1,0:T(8,128)(2,1)S(1)}, bf16[64,1024]{1,0:T(8,128)(2,1)S(1)}, u32[]{:S(2)}, u32[]{:S(2)}) collective-permute-start(bf16[64,1024]{1,0:T(8,128)(2,1)S(1)} %get-tuple-element.73), channel_id=1, source_target_pairs={{0,8},{4,12},{8,0},{12,4},{16,24},{20,28},{24,16},{28,20},{1,9},{5... | collective-permute-start | bytes 393224 | tf_op jit(solution)/shard_map/ppermute | solution.py:335
  72.0 7.1 %collective-permute-start.8 = (bf16[64,1024]{1,0:T(8,128)(2,1)S(1)}, bf16[64,1024]{1,0:T(8,128)(2,1)S(1)}, u32[]{:S(2)}, u32[]{:S(2)}) collective-permute-start(bf16[64,1024]{1,0:T(8,128)(2,1)S(1)} %get-tuple-element.74), channel_id=1, source_target_pairs={{0,16},{4,20},{8,24},{12,28},{16,0},{20,4},{24,8},{28,12},{1,17},{... | collective-permute-start | bytes 393224 | tf_op jit(solution)/shard_map/ppermute | solution.py:335
  72.8 6.3 %collective-permute-start.9 = (bf16[64,1024]{1,0:T(8,128)(2,1)S(1)}, bf16[64,1024]{1,0:T(8,128)(2,1)S(1)}, u32[]{:S(2)}, u32[]{:S(2)}) collective-permute-start(bf16[64,1024]{1,0:T(8,128)(2,1)S(1)} %get-tuple-element.75), channel_id=1, source_target_pairs={{0,24},{4,28},{8,16},{12,20},{16,8},{20,12},{24,0},{28,4},{1,25},{... | collective-permute-start | bytes 393224 | tf_op jit(solution)/shard_map/ppermute | solution.py:335
  85.7 9.7 %collective-permute-start.21 = (bf16[64,1024]{1,0:T(8,128)(2,1)S(1)}, bf16[64,1024]{1,0:T(8,128)(2,1)S(1)}, u32[]{:S(2)}, u32[]{:S(2)}) collective-permute-start(bf16[64,1024]{1,0:T(8,128)(2,1)S(1)} %get-tuple-element.105), channel_id=1, source_target_pairs={{0,8},{4,12},{8,0},{12,4},{16,24},{20,28},{24,16},{28,20},{1,9},{5... | collective-permute-start | bytes 393224 | tf_op jit(solution)/shard_map/ppermute | solution.py:296
  87.4 9.1 %collective-permute-start.23 = (bf16[64,1024]{1,0:T(8,128)(2,1)S(1)}, bf16[64,1024]{1,0:T(8,128)(2,1)S(1)}, u32[]{:S(2)}, u32[]{:S(2)}) collective-permute-start(bf16[64,1024]{1,0:T(8,128)(2,1)S(1)} %get-tuple-element.107), channel_id=1, source_target_pairs={{0,16},{4,20},{8,24},{12,28},{16,0},{20,4},{24,8},{28,12},{1,17},{... | collective-permute-start | bytes 393224 | tf_op jit(solution)/shard_map/ppermute | solution.py:296
  87.9 9.0 %collective-permute-start.25 = (bf16[64,1024]{1,0:T(8,128)(2,1)S(1)}, bf16[64,1024]{1,0:T(8,128)(2,1)S(1)}, u32[]{:S(2)}, u32[]{:S(2)}) collective-permute-start(bf16[64,1024]{1,0:T(8,128)(2,1)S(1)} %get-tuple-element.109), channel_id=1, source_target_pairs={{0,24},{4,28},{8,16},{12,20},{16,8},{20,12},{24,0},{28,4},{1,25},{... | collective-permute-start | bytes 393224 | tf_op jit(solution)/shard_map/ppermute | solution.py:296
  89.2 7.7 %collective-permute-start.26 = (bf16[64,1024]{1,0:T(8,128)(2,1)S(1)}, bf16[64,1024]{1,0:T(8,128)(2,1)S(1)}, u32[]{:S(2)}, u32[]{:S(2)}) collective-permute-start(bf16[64,1024]{1,0:T(8,128)(2,1)S(1)} %get-tuple-element.110), channel_id=1, source_target_pairs={{0,28},{4,24},{8,20},{12,16},{16,12},{20,8},{24,4},{28,0},{1,29},{... | collective-permute-start | bytes 393224 | tf_op jit(solution)/shard_map/ppermute | solution.py:296
  (3 other events, 14.1 us)

commit v2 on v1

--- a/solution.py
+++ b/solution.py
@@ -11,6 +11,7 @@
 
 HEADS = 8
 CHUNKS = 2
+PIECES = 4
 BF = jnp.bfloat16
 F32 = jnp.float32
 
@@ -73,13 +74,12 @@
     after = (load() + dot(mixed[...], wo[...])).astype(BF)
     o = lax.broadcasted_iota(jnp.int32, (tokens, 1), 0)
     i, jj, rest = o % rows, (o // rows) % cpd, o // (rows * cpd)
-    chips = nr // 2
     if len(outs) == nc:
-        k, b, q = rest // nr, (rest // chips) % 2, rest % chips
+        k, b, q = rest // nr, (rest // (nr // 2)) % 2, rest % (nr // 2)
+        r = jnp.bitwise_xor(2 * q + b, lax.axis_index("row"))
     else:
-        k, b, q = rest % nc, rest // (nc * chips), (rest // nc) % chips
-    m = 2 * q + b
-    source = (i * nc + k) * cols + cpd * jnp.bitwise_xor(m, lax.axis_index("row")) + jj
+        r, k = rest // nc, jnp.bitwise_xor(rest % nc, lax.axis_index("col"))
+    source = (i * nc + k) * cols + cpd * r + jj
     moved = dot(one_hot(source, tokens), after).astype(BF)
     each = tokens // len(outs)
     for part, out in enumerate(outs):
@@ -90,22 +90,21 @@
     return pltpu.with_memory_space_constraint(x, pltpu.VMEM)
 
 
-SMEM_SPEC = pl.BlockSpec(memory_space=pltpu.SMEM)
+HBM_SPEC = pl.BlockSpec(memory_space=pltpu.HBM)
 VMEM_SPEC = pl.BlockSpec(memory_space=pltpu.VMEM)
 
 
-def call(kernel, ins, outs, scratch, flops, limit=16 << 20):
+def call(kernel, ins, outs, scratch, flops, limit=16 << 20, far=False):
     moved = sum(a.size * 2 for a in ins) + sum(math.prod(o) * 2 for o in outs)
-    small = [a.dtype == jnp.int32 for a in ins]
     return pl.pallas_call(
         kernel,
-        in_specs=[SMEM_SPEC if i else VMEM_SPEC for i in small],
+        in_specs=[VMEM_SPEC] * len(ins),
         out_specs=[VMEM_SPEC] * len(outs),
         out_shape=[jax.ShapeDtypeStruct(o, BF) for o in outs],
         scratch_shapes=scratch,
         compiler_params=pltpu.CompilerParams(vmem_limit_bytes=limit),
         cost_estimate=pl.CostEstimate(flops=flops, bytes_accessed=moved, transcendentals=0),
-    )(*[a if i else near(a) for a, i in zip(ins, small)])
+    )(*[a if far else near(a) for a in ins])
 
 
 def split_kernel(count, band, offset, latents, *refs):
@@ -177,44 +176,27 @@
 
 
 def gather_columns(g, xs, by_row):
-    cpd, rows, nr, nc = g["cpd"], g["rows"], g["nr"], g["nc"]
+    cpd, rows, nc = g["cpd"], g["rows"], g["nc"]
     x = jnp.concatenate([ref[...] for ref in xs], 0)
     tokens = x.shape[0]
     o = lax.broadcasted_iota(jnp.int32, (tokens, 1), 0)
     per = tokens // cpd
     jj, mk, i = o // per, (o % per) // rows, o % rows
     if not by_row:
-        mk = (mk % nc) * nr + mk // nc
+        r, c = lax.axis_index("row"), lax.axis_index("col")
+        mk = jnp.bitwise_xor(mk // nc, r) * nc + jnp.bitwise_xor(mk % nc, c)
     return dot(one_hot((mk * cpd + jj) * rows + i, tokens), x)
 
 
-def project_kernel(g, by_row, *refs):
-    xs, w, outs, x_out = refs[:-5], refs[-5], refs[-4:-1], refs[-1]
-    x = gather_columns(g, xs, by_row)
-    x_out[...] = x.astype(BF)
-    n = normalize(x)
-    width = n.shape[-1]
-    for j, out in enumerate(outs):
-        out[...] = dot(n, w[:, j * width : (j + 1) * width]).astype(BF)
-
-
-def project_stage(g, slots, col_qkv, by_row):
-    width = col_qkv.shape[0]
-    tokens = sum(a.shape[0] for a in slots)
-    return call(
-        functools.partial(project_kernel, g, by_row),
-        [*slots, col_qkv],
-        [(tokens, width)] * 4,
-        [],
-        6 * tokens * width * width,
-    )
-
-
 def group_kernel(g, members, *refs):
+    old, (wo, up, down) = refs[: 4 * CHUNKS], refs[4 * CHUNKS : 4 * CHUNKS + 3]
+    outs, (mixed, hidden) = refs[4 * CHUNKS + 3 : -2], refs[-2:]
+    group_body(g, members, old, wo, outs, mixed, lambda: None, lambda after: feed_forward(after, up, down, hidden))
+
+
+def group_body(g, members, old, wo, outs, mixed, ready, finish):
     nr, cpd, nc, rows = g["nr"], g["cpd"], g["nc"], g["rows"]
-    old, (wo, up, down) = refs[: 4 * CHUNKS], refs[4 * CHUNKS : 4 * CHUNKS + 3]
     count = len(members)
-    outs, (mixed, hidden) = refs[4 * CHUNKS + 3 :][:count], refs[4 * CHUNKS + 3 + count :]
     per = old[0].shape[0] // cpd
     each = per // nr
     width = wo.shape[0]
@@ -236,60 +218,172 @@
     size = CHUNKS * count * each
     for (jj, lanes), out in zip(where, attend(units, None)):
         mixed[jj * size : (jj + 1) * size, lanes] = out
+    ready()
     base = jnp.concatenate([queries(3, slice(0, width), jj) for jj in range(cpd)], 0)
     after = (base.astype(F32) + dot(mixed[...], wo[...])).astype(BF)
-    n = normalize(after.astype(F32))
-    block = min(512, up.shape[1])
-    for b in range(0, up.shape[1], block):
-        hidden[:, b : b + block] = jax.nn.gelu(dot(n, up[:, b : b + block]), approximate=True).astype(BF)
-    result = (after.astype(F32) + dot(hidden[...], down[...])).astype(BF)
-    tokens = result.shape[0]
+    after = finish(after)
+    tokens = after.shape[0]
     o = lax.broadcasted_iota(jnp.int32, (tokens, 1), 0)
     jj, i, t = o % cpd, (o // cpd) % rows, (o // (cpd * rows)) % CHUNKS
     c, m = (o // (cpd * rows * CHUNKS)) % nc, o // (cpd * rows * CHUNKS * nc)
     k = jnp.bitwise_xor(c, lax.axis_index("col"))
     source = (((jj * CHUNKS + t) * count + m) * nc + k) * rows + i
-    moved = dot(one_hot(source, tokens), result).astype(BF)
+    moved = dot(one_hot(source, tokens), after).astype(BF)
     size = tokens // count
     for m in range(count):
         outs[m][...] = moved[m * size : (m + 1) * size, :]
 
 
 def group_stage(g, members, old, col_out, up_weight, down_weight):
-    width, hidden = up_weight.shape
+    width, size = up_weight.shape
     count = len(members)
-    size = CHUNKS * old[0].shape[0] // g["nr"]
-    tokens = count * size
+    each = CHUNKS * old[0].shape[0] // g["nr"]
+    tokens = count * each
     return call(
         functools.partial(group_kernel, g, members),
         [*old, col_out, up_weight, down_weight],
-        [(size, width)] * count,
-        [pltpu.VMEM((tokens, width), BF), pltpu.VMEM((tokens, hidden), BF)],
-        4 * tokens * width * hidden,
+        [(each, width)] * count,
+        [pltpu.VMEM((tokens, width), BF), pltpu.VMEM((tokens, size), BF)],
+        4 * tokens * width * size,
     )
 
 
-def final_kernel(g, *refs):
-    nr, cpd, cols, span = g["nr"], g["cpd"], g["cols"], g["span"]
-    ins, out = refs[:nr], refs[nr]
+def finish_kernel(g, members, counts, *refs):
+    n_x = sum(counts)
+    xs, far_qkv, far_weights, rest = refs[:n_x], refs[n_x], refs[n_x + 1 : n_x + 4], refs[n_x + 4 :]
+    old, weights, outs = rest[: 4 * CHUNKS], rest[4 * CHUNKS : 4 * CHUNKS + 3], rest[4 * CHUNKS + 3 : -3]
+    qkv, mixed, sems = rest[-3:]
+    width = xs[0].shape[1]
+    sources = [far_qkv.at[:, pl.ds(j * width, width)] for j in range(3)] + list(far_weights)
+    targets = [qkv.at[:, pl.ds(j * width, width)] for j in range(3)] + list(weights)
+
+    def pieces(i):
+        size = sources[i].shape[0] // PIECES
+        spans = [pl.ds(a * size, size) for a in range(PIECES)]
+        return [pltpu.make_async_copy(sources[i].at[a], targets[i].at[a], sems.at[i, p]) for p, a in enumerate(spans)]
+
+    def begin(*which):
+        for i in which:
+            for copy in pieces(i):
+                copy.start()
+
+    def arrived(i):
+        for copy in pieces(i):
+            copy.wait()
+
+    begin(0, 1)
+    normed, at = [], 0
+    for t, count in enumerate(counts):
+        x = gather_columns(g, xs[at : at + count], t < CHUNKS - 1)
+        old[4 * t + 3][...] = x.astype(BF)
+        normed.append(normalize(x))
+        at += count
+    n = jnp.concatenate(normed, 0)
+    size = n.shape[0] // CHUNKS
+    for j in range(3):
+        arrived(j)
+        begin(*([2], [3, 4], [5])[j])
+        value = dot(n, qkv[:, j * width : (j + 1) * width]).astype(BF)
+        for t in range(CHUNKS):
+            old[4 * t + j][...] = value[t * size : (t + 1) * size, :]
+
+    group_body(g, members, old, weights[0], outs, mixed, lambda: arrived(3), lambda after: after)
+    arrived(4)
+    arrived(5)
+
+
+def finish_stage(g, members, slots, col_qkv, col_out, up_weight, down_weight):
+    width = col_out.shape[0]
+    count = len(members)
+    chunk = sum(a.shape[0] for a in slots[0])
+    tokens = count * CHUNKS * chunk // g["nr"]
+    far = [col_qkv, col_out, up_weight, down_weight]
+    flat = [a for part in slots for a in part]
+    kept = [(chunk, width)] * (4 * CHUNKS) + [col_out.shape, up_weight.shape, down_weight.shape]
+    outs = pl.pallas_call(
+        functools.partial(finish_kernel, g, members, [len(part) for part in slots]),
+        in_specs=[VMEM_SPEC] * len(flat) + [HBM_SPEC] * len(far),
+        out_specs=[VMEM_SPEC] * (len(kept) + count),
+        out_shape=[pltpu.VMEM(shape, BF) for shape in kept] + [jax.ShapeDtypeStruct((tokens // count, width), BF)] * count,
+        scratch_shapes=[
+            pltpu.VMEM(col_qkv.shape, BF),
+            pltpu.VMEM((tokens, width), BF),
+            pltpu.SemaphoreType.DMA((6, PIECES)),
+        ],
+        compiler_params=pltpu.CompilerParams(vmem_limit_bytes=28 << 20),
+        cost_estimate=pl.CostEstimate(flops=16 * tokens * width * width, bytes_accessed=2 * sum(a.size for a in far), transcendentals=0),
+        name="finish_stage",
+    )(*[near(a) for a in flat], *[pltpu.with_memory_space_constraint(a, pltpu.HBM) for a in far])
+    return outs[: 4 * CHUNKS], outs[4 * CHUNKS : 4 * CHUNKS + 3], outs[4 * CHUNKS + 3 :]
+
+
+def feed_forward(x, up, down, hidden):
+    n = normalize(x.astype(F32))
+    block = min(512, up.shape[1])
+    for b in range(0, up.shape[1], block):
+        hidden[:, b : b + block] = jax.nn.gelu(dot(n, up[:, b : b + block]), approximate=True).astype(BF)
+    return (x.astype(F32) + dot(hidden[...], down[...])).astype(BF)
+
+
+def ffn_kernel(*refs):
+    slots, (up, down, out, hidden) = refs[:-4], refs[-4:]
+    out[...] = feed_forward(jnp.concatenate([ref[...] for ref in slots], 0), up, down, hidden)
+
+
+def ffn_stage(slots, up_weight, down_weight):
+    width, size = up_weight.shape
+    tokens = sum(a.shape[0] for a in slots)
+    (out,) = call(
+        ffn_kernel,
+        [*slots, up_weight, down_weight],
+        [(tokens, width)],
+        [pltpu.VMEM((tokens, size), BF)],
+        4 * tokens * width * size,
+    )
+    return out
+
+
+def final_kernel(g, order, *refs):
+    cpd, cols, span = g["cpd"], g["cols"], g["span"]
+    first, slots, (out, held, sems) = refs[0], refs[1:-3], refs[-3:]
     tokens = span * cols
+    each = slots[0].shape[0]
     o = lax.broadcasted_iota(jnp.int32, (tokens, 1), 0)
     w, j = o // cols, o % cols
     m = jnp.bitwise_xor(j // cpd, lax.axis_index("row"))
     pick = one_hot((m * span + w) * cpd + j % cpd, tokens)
-    rows = ins[0].shape[0] // cpd
-    for a in range(0, rows, span):
-        x = jnp.concatenate([ref[a * cpd : (a + span) * cpd, :] for ref in ins], 0)
-        out[a * cols : (a + span) * cols, :] = dot(pick, x).astype(BF)
-
-
-def final_stage(g, slots):
-    each, width = slots[0].shape
-    total = g["nr"] * each
-    (out,) = call(
-        functools.partial(final_kernel, g), [*slots], [(total, width)], [], 2 * total * width * g["span"] * g["cols"]
-    )
-    return out
+    half = len(order) - len(slots)
+    copies = []
+    for a in range(0, each // cpd, span):
+        parts = []
+        for m in range(len(order)):
+            i = order.index(m)
+            at, ref = (i * each, first) if i < half else (0, slots[i - half])
+            parts.append(ref[at + a * cpd : at + (a + span) * cpd, :])
+        held[a * cols : (a + span) * cols, :] = dot(pick, jnp.concatenate(parts, 0)).astype(BF)
+        rows = pl.ds(a * cols, span * cols)
+        copies.append(pltpu.make_async_copy(held.at[rows], out.at[rows], sems.at[len(copies)]))
+        copies[-1].start()
+    for copy in copies:
+        copy.wait()
+
+
+def final_stage(g, order, first, slots):
+    width = first.shape[1]
+    tokens = first.shape[0] + sum(a.shape[0] for a in slots)
+    return pl.pallas_call(
+        functools.partial(final_kernel, g, order),
+        in_specs=[VMEM_SPEC] * (1 + len(slots)),
+        out_specs=HBM_SPEC,
+        out_shape=pltpu.HBM((tokens, width), BF),
+        scratch_shapes=[
+            pltpu.VMEM((tokens, width), BF),
+            pltpu.SemaphoreType.DMA((tokens // (g["span"] * g["cols"]),)),
+        ],
+        compiler_params=pltpu.CompilerParams(vmem_limit_bytes=8 << 20),
+        cost_estimate=pl.CostEstimate(flops=0, bytes_accessed=4 * tokens * width, transcendentals=0),
+        name="final_stage",
+    )(*[near(a) for a in [first, *slots]])
 
 
 def swap(x, axis, size, k):
@@ -316,7 +410,7 @@
 
 def deal(ins, plan):
     width = ins[0].shape[1]
-    return call(functools.partial(deal_kernel, plan), ins, [(sum(p[2] for p in pieces), width) for pieces in plan], [], 0)
+    return call(functools.partial(deal_kernel, plan), ins, [(sum(p[2] for p in pieces), width) for pieces in plan], [], 0, far=True)
 
 
 def row_hop(ins, own, sent, cells, nr):
@@ -352,12 +446,11 @@
         return exchange(slots, "col", z_order)
 
     first = enter(0, latents)
-    weights = fetch([row_qkv, row_out, col_qkv, col_out])
-    latents, row_qkv, row_out, col_qkv, col_out = lax.optimization_barrier((latents, *weights))
+    weights = fetch([row_qkv, row_out])
+    latents, row_qkv, row_out = lax.optimization_barrier((latents, *weights))
     second = enter(1, latents)
 
     parts = row_stage(g, nc, first, row_qkv, row_out)
-    up_weight, down_weight = fetch([up_weight, down_weight])
     parts = exchange(parts, "col", z_order)
     half = chips * cell
     (sent,) = deal(parts, [[(k, half, half) for k in range(nc)]])
@@ -369,21 +462,24 @@
         nr,
     )
 
-    stay, sent = row_stage(g, 2, second, row_qkv, row_out)
-    size = nc * cell
-    parts = row_hop([stay], lambda q: [(0, q * size, size)], sent, lambda q: [(q * size, size)], nr)
-    plan = [[(q, b * size + k * cell, cell) for q in range(chips) for b in range(2)] for k in range(nc)]
-    parts = deal(parts, plan)
-    slots1 = exchange(parts, "col", z_order)
-
-    old = project_stage(g, slots0, col_qkv, True)
-    old += project_stage(g, slots1, col_qkv, False)
-    final = [None] * nr
-    for members in groups(nr):
-        outs = group_stage(g, members, old, col_out, up_weight, down_weight)
+    (parts,) = row_stage(g, 1, second, row_qkv, row_out)
+    parts = parts.reshape(nr * nc, cell, width)
+    parts = lax.all_to_all(parts, ("row", "col"), split_axis=0, concat_axis=0, tiled=True)
+    slots1 = parts.reshape(nr * nc * cell, width)
+
+    came = {}
+    near_half, far_half = groups(nr)
+    for b, members in enumerate((near_half, far_half)):
+        if b == 0:
+            ins = [slots0, [slots1]]
+            old, weights, outs = finish_stage(g, members, ins, col_qkv, col_out, up_weight, down_weight)
+        else:
+            outs = group_stage(g, members, old, *weights)
         for m, out in zip(members, outs):
-            final[m] = swap(out, "row", nr, m)
-    return final_stage(g, final).reshape(local_rows, cols, width)
+            came[m] = swap(out, "row", nr, m)
+    done = ffn_stage([came[m] for m in near_half], *weights[1:])
+    out = final_stage(g, near_half + far_half, done, [came[m] for m in far_half])
+    return out.reshape(local_rows, cols, width)
 
 
 def chip_order(nr):

time: 103 us -> 113 us (1.097)
  waiting for transfers between devices: 35.8 us -> 48.1 us
  starting transfers between devices: 34.2 us -> 31.1 us
  local copies, waits for them, and re-layouts: 0 us -> 2.79 us
  Pallas kernels: 32.8 us -> 30.3 us
    ppermute x21 -> x17, waiting for transfers between devices: 29.4 us -> 42.1 us  [swap(): lax.ppermute(x, axis, [(i, i ^ k) for i in range(size)])]
    pallas_call x2 -> x1, Pallas kernels: 9.36 us -> 3.43 us  [fetch(): pl.pallas_call(functools.partial(fetch_kernel, count, pieces), in_specs=[...]
    all_to_all x0 -> x1, starting transfers between devices: none -> 5.43 us  [on_device(): lax.all_to_all(parts, ('row', 'col'), split_axis=0, concat_axis=0, tiled=...]
    ppermute x21 -> x17, starting transfers between devices: 27.1 us -> 22.1 us  [swap(): lax.ppermute(x, axis, [(i, i ^ k) for i in range(size)])]
    ppermute x6 -> x3, starting transfers between devices: 7.11 us -> 3.55 us  [spread(): lax.ppermute(parts[q], 'row', [(i, i ^ 2 * q) for i in range(2 * n)])]
    unnamed x0 -> x4, local copies, waits for them, and re-layouts: none -> 2.79 us
    pallas_call x11 -> x8, Pallas kernels: 21.2 us -> 24 us  [the longest x6 14.7 us: call(): pl.pallas_call(kernel, in_specs=[VMEM_SPEC] * len(ins), out_specs=[VMEM_S...]
    ppermute x6 -> x3, waiting for transfers between devices: 6.43 us -> 5.93 us  [spread(): lax.ppermute(parts[q], 'row', [(i, i ^ 2 * q) for i in range(2 * n)])]
  transfers between devices with their start and end apart: 27 -> 21, of which waited for: 9 -> 11; matrix products, arithmetic and copies ran while one was open for 0% -> 0% of each run, Pallas kernels for 17% -> 10%
where the time goes in v2:
time: 113 us
  waiting for transfers between devices  48.1 us (43%)
  starting transfers between devices  31.1 us (28%)
  Pallas kernels  30.3 us (27%)
  local copies, waits for them, and re-layouts  2.79 us (2%)
    ppermute x17, waiting for transfers between devices, swap(): lax.ppermute(x, axis, [(i, i ^ k) for i in range(size)])  42.1 us
    ppermute x17, starting transfers between devices, swap(): lax.ppermute(x, axis, [(i, i ^ k) for i in range(size)])  22.1 us
    pallas_call x6, Pallas kernels, call(): pl.pallas_call(kernel, in_specs=[VMEM_SPEC] * len(ins), out_specs=[VMEM_S...  14.7 us
    pallas_call x1, Pallas kernels, finish_stage(): pl.pallas_call(functools.partial(finish_kernel, g, members, [len(part) fo...  8.07 us
    ppermute x3, waiting for transfers between devices, spread(): lax.ppermute(parts[q], 'row', [(i, i ^ 2 * q) for i in range(2 * n)])  5.93 us
    all_to_all x1, starting transfers between devices, on_device(): lax.all_to_all(parts, ('row', 'col'), split_axis=0, concat_axis=0, tiled=...  5.43 us
    ppermute x3, starting transfers between devices, spread(): lax.ppermute(parts[q], 'row', [(i, i ^ 2 * q) for i in range(2 * n)])  3.55 us
    pallas_call x1, Pallas kernels, fetch(): pl.pallas_call(functools.partial(fetch_kernel, count, pieces), in_specs=[...  3.43 us
  transfers between devices with their start and end apart: 21, of which 11 were waited for; matrix products, arithmetic and copies ran while one was open for 0% of the time, Pallas kernels for 10%

profile of v2, /device:TPU:0, one launch (start us, length us, event | category | flops | bytes accessed | tf_op | source)
XLA Modules:
  0.0 112.6 jit_solution(2509709379361067108)
XLA Ops:
  0.0 3.4 %fetch.1 = (bf16[1024,3072]{1,0:T(8,128)(2,1)S(1)}, bf16[1024,1024]{1,0:T(8,128)(2,1)S(1)}) custom-call(bf16[1024,3072]{1,0:T(8,128)(2,1)} %refs_0_.1, bf16[1024,1024]{1,0:T(8,128)(2,1)} %refs_1_.1), custom_call_target="tpu_custom_call" | custom-call | bytes 16777216 | tf_op jit(solution)/shard_map/fetch/pallas_call | solution.py:154
  3.4 1.8 %split.3 = (bf16[4,16,1024]{2,1,0:T(8,128)(2,1)S(1)}, bf16[4,16,1024]{2,1,0:T(8,128)(2,1)S(1)}, bf16[4,16,1024]{2,1,0:T(8,128)(2,1)S(1)}, bf16[4,16,1024]{2,1,0:T(8,128)(2,1)S(1)}) custom-call(bf16[32,16,1024]{2,1,0:T(8,128)(2,1)} %latents.2), custom_call_target="tpu_custom_call" | custom-call | bytes 1048576 | tf_op jit(solution)/shard_map/split/pallas_call | solution.py:125
  5.2 3.1 %collective-permute-start.10 = (bf16[64,1024]{1,0:T(8,128)(2,1)S(1)}, bf16[64,1024]{1,0:T(8,128)(2,1)S(1)}, u32[]{:S(2)}, u32[]{:S(2)}) collective-permute-start(bf16[64,1024]{1,0:T(8,128)(2,1)S(1)} %bitcast.18), channel_id=1, source_target_pairs={{0,1},{1,0},{2,3},{3,2},{4,5},{5,4},{6,7},{7,6},{8,9},{9,8},{10,11... | collective-permute-start | bytes 393224 | tf_op jit(solution)/shard_map/ppermute | solution.py:390
  8.4 2.6 %collective-permute-start.11 = (bf16[64,1024]{1,0:T(8,128)(2,1)S(1)}, bf16[64,1024]{1,0:T(8,128)(2,1)S(1)}, u32[]{:S(2)}, u32[]{:S(2)}) collective-permute-start(bf16[64,1024]{1,0:T(8,128)(2,1)S(1)} %bitcast.16), channel_id=1, source_target_pairs={{0,2},{1,3},{2,0},{3,1},{4,6},{5,7},{6,4},{7,5},{8,10},{9,11},{10,... | collective-permute-start | bytes 393224 | tf_op jit(solution)/shard_map/ppermute | solution.py:390
  10.9 2.5 %collective-permute-done.10.refs_1_ = bf16[64,1024]{1,0:T(8,128)(2,1)S(1)} collective-permute-done((bf16[64,1024]{1,0:T(8,128)(2,1)S(1)}, bf16[64,1024]{1,0:T(8,128)(2,1)S(1)}, u32[]{:S(2)}, u32[]{:S(2)}) %collective-permute-start.10) | collective-permute-done | bytes 131104 | tf_op jit(solution)/shard_map/ppermute | solution.py:390
  13.4 7.8 %collective-permute-done.11.refs_2_ = bf16[64,1024]{1,0:T(8,128)(2,1)S(1)} collective-permute-done((bf16[64,1024]{1,0:T(8,128)(2,1)S(1)}, bf16[64,1024]{1,0:T(8,128)(2,1)S(1)}, u32[]{:S(2)}, u32[]{:S(2)}) %collective-permute-start.11) | collective-permute-done | bytes 131104 | tf_op jit(solution)/shard_map/ppermute | solution.py:390
  21.2 4.1 %shard_map.76 = bf16[256,1024]{1,0:T(8,128)(2,1)} custom-call(bf16[64,1024]{1,0:T(8,128)(2,1)S(1)} %bitcast.13, bf16[64,1024]{1,0:T(8,128)(2,1)S(1)} %collective-permute-done.10.refs_1_, bf16[64,1024]{1,0:T(8,128)(2,1)S(1)} %collective-permute-done.11.refs_2_, bf16[64,1024]{1,0:T(8,128)(2,1)S(1)} %collective-permute-done.12.refs_3_, ...), custom_call_target="tpu_custom_call" | custom-call | flops 2147483648 | bytes 9437184 | tf_op jit(solution)/shard_map/pallas_call | solution.py:99
  25.4 5.4 %all-to-all-start = ((bf16[32,8,1024]{2,1,0:T(8,128)(2,1)}), bf16[32,8,1024]{2,1,0:T(8,128)(2,1)S(1)}, u32[]{:S(2)}, u32[]{:S(2)}) async-start(bf16[32,8,1024]{2,1,0:T(8,128)(2,1)} %bitcast.8), calls=%async_computation | async-start | bytes 1048576 | tf_op jit(solution)/shard_map/all_to_all | solution.py:467
  32.0 1.8 %collective-permute-start = (bf16[64,1024]{1,0:T(8,128)(2,1)S(1)}, bf16[64,1024]{1,0:T(8,128)(2,1)S(1)}, u32[]{:S(2)}, u32[]{:S(2)}) collective-permute-start(bf16[64,1024]{1,0:T(8,128)(2,1)S(1)} %bitcast.19), channel_id=1, source_target_pairs={{0,1},{1,0},{2,3},{3,2},{4,5},{5,4},{6,7},{7,6},{8,9},{9,8},{10,11... | collective-permute-start | bytes 393224 | tf_op jit(solution)/shard_map/ppermute | solution.py:390
  33.8 2.4 %collective-permute-start.1 = (bf16[64,1024]{1,0:T(8,128)(2,1)S(1)}, bf16[64,1024]{1,0:T(8,128)(2,1)S(1)}, u32[]{:S(2)}, u32[]{:S(2)}) collective-permute-start(bf16[64,1024]{1,0:T(8,128)(2,1)S(1)} %bitcast.17), channel_id=1, source_target_pairs={{0,2},{1,3},{2,0},{3,1},{4,6},{5,7},{6,4},{7,5},{8,10},{9,11},{10,... | collective-permute-start | bytes 393224 | tf_op jit(solution)/shard_map/ppermute | solution.py:390
  36.4 7.6 %collective-permute-done.refs_1_ = bf16[64,1024]{1,0:T(8,128)(2,1)S(1)} collective-permute-done((bf16[64,1024]{1,0:T(8,128)(2,1)S(1)}, bf16[64,1024]{1,0:T(8,128)(2,1)S(1)}, u32[]{:S(2)}, u32[]{:S(2)}) %collective-permute-start) | collective-permute-done | bytes 131104 | tf_op jit(solution)/shard_map/ppermute | solution.py:390
  44.0 10.6 %collective-permute-done.1.refs_2_ = bf16[64,1024]{1,0:T(8,128)(2,1)S(1)} collective-permute-done((bf16[64,1024]{1,0:T(8,128)(2,1)S(1)}, bf16[64,1024]{1,0:T(8,128)(2,1)S(1)}, u32[]{:S(2)}, u32[]{:S(2)}) %collective-permute-start.1) | collective-permute-done | bytes 131104 | tf_op jit(solution)/shard_map/ppermute | solution.py:390
  54.6 2.8 %copy-done.1 = bf16[1024,3072]{1,0:T(8,128)(2,1)S(1)} copy-done((bf16[1024,3072]{1,0:T(8,128)(2,1)S(1)}, bf16[1024,3072]{1,0:T(8,128)(2,1)}, u32[]{:S(2)}) %copy-start.1) | copy-done | bytes 6291480
  57.4 3.3 %shard_map.73 = (bf16[64,1024]{1,0:T(8,128)(2,1)S(1)}, bf16[64,1024]{1,0:T(8,128)(2,1)S(1)}, bf16[64,1024]{1,0:T(8,128)(2,1)S(1)}, bf16[64,1024]{1,0:T(8,128)(2,1)S(1)}) custom-call(bf16[64,1024]{1,0:T(8,128)(2,1)S(1)} %bitcast.12, bf16[64,1024]{1,0:T(8,128)(2,1)S(1)} %collective-permute-done.refs_1_, bf16[64,1024]{1,0:T(8,128)(2,1)S(1)} %collective-permute-done.1.refs_2_, ...), custom_call_target="tpu_custom_call" | custom-call | flops 2147483648 | bytes 9437184 | tf_op jit(solution)/shard_map/pallas_call | solution.py:99
  60.7 2.9 %collective-permute-start.3 = (bf16[64,1024]{1,0:T(8,128)(2,1)S(1)}, bf16[64,1024]{1,0:T(8,128)(2,1)S(1)}, u32[]{:S(2)}, u32[]{:S(2)}) collective-permute-start(bf16[64,1024]{1,0:T(8,128)(2,1)S(1)} %get-tuple-element.54), channel_id=1, source_target_pairs={{0,1},{1,0},{2,3},{3,2},{4,5},{5,4},{6,7},{7,6},{8,9},{9,8},{10,11... | collective-permute-start | bytes 393224 | tf_op jit(solution)/shard_map/ppermute | solution.py:390
  63.7 2.4 %collective-permute-start.5 = (bf16[64,1024]{1,0:T(8,128)(2,1)S(1)}, bf16[64,1024]{1,0:T(8,128)(2,1)S(1)}, u32[]{:S(2)}, u32[]{:S(2)}) collective-permute-start(bf16[64,1024]{1,0:T(8,128)(2,1)S(1)} %get-tuple-element.56), channel_id=1, source_target_pairs={{0,3},{1,2},{2,1},{3,0},{4,7},{5,6},{6,5},{7,4},{8,11},{9,10},{10,... | collective-permute-start | bytes 393224 | tf_op jit(solution)/shard_map/ppermute | solution.py:390
  66.0 2.1 %collective-permute-done.3.refs_1_ = bf16[64,1024]{1,0:T(8,128)(2,1)S(1)} collective-permute-done((bf16[64,1024]{1,0:T(8,128)(2,1)S(1)}, bf16[64,1024]{1,0:T(8,128)(2,1)S(1)}, u32[]{:S(2)}, u32[]{:S(2)}) %collective-permute-start.3) | collective-permute-done | bytes 131104 | tf_op jit(solution)/shard_map/ppermute | solution.py:390
  68.2 8.0 %collective-permute-done.4.refs_2_ = bf16[64,1024]{1,0:T(8,128)(2,1)S(1)} collective-permute-done((bf16[64,1024]{1,0:T(8,128)(2,1)S(1)}, bf16[64,1024]{1,0:T(8,128)(2,1)S(1)}, u32[]{:S(2)}, u32[]{:S(2)}) %collective-permute-start.4) | collective-permute-done | bytes 131104 | tf_op jit(solution)/shard_map/ppermute | solution.py:390
  81.3 2.6 %collective-permute-done.7.refs_1_ = bf16[64,1024]{1,0:T(8,128)(2,1)S(1)} collective-permute-done((bf16[64,1024]{1,0:T(8,128)(2,1)S(1)}, bf16[64,1024]{1,0:T(8,128)(2,1)S(1)}, u32[]{:S(2)}, u32[]{:S(2)}) %collective-permute-start.7) | collective-permute-done | bytes 131104 | tf_op jit(solution)/shard_map/ppermute | solution.py:429
  84.0 3.3 %collective-permute-done.8.refs_2_ = bf16[64,1024]{1,0:T(8,128)(2,1)S(1)} collective-permute-done((bf16[64,1024]{1,0:T(8,128)(2,1)S(1)}, bf16[64,1024]{1,0:T(8,128)(2,1)S(1)}, u32[]{:S(2)}, u32[]{:S(2)}) %collective-permute-start.8) | collective-permute-done | bytes 131104 | tf_op jit(solution)/shard_map/ppermute | solution.py:429
  87.3 8.1 %finish_stage.1 = (bf16[256,1024]{1,0:T(8,128)(2,1)S(1)}, bf16[256,1024]{1,0:T(8,128)(2,1)S(1)}, bf16[256,1024]{1,0:T(8,128)(2,1)S(1)}, bf16[256,1024]{1,0:T(8,1...) custom-call(bf16[64,1024]{1,0:T(8,128)(2,1)S(1)} %get-tuple-element., ...), custom_call_target="tpu_custom_call" | custom-call | flops 4294967296 | bytes 16777216 | tf_op jit(solution)/shard_map/finish_stage/pallas_call | solution.py:303
  98.9 4.5 %shard_map.78 = (bf16[64,1024]{1,0:T(8,128)(2,1)S(1)}, bf16[64,1024]{1,0:T(8,128)(2,1)S(1)}, bf16[64,1024]{1,0:T(8,128)(2,1)S(1)}, bf16[64,1024]{1,0:T(8,128)(2,1)S(1)}) custom-call(bf16[256,1024]{1,0:T(8,128)(2,1)S(1)} %get-tuple-element.72.refs_0_, bf16[256,1024]{1,0:T(8,128)(2,1)S(1)} %get-tuple-element.73.refs_1_, ...), custom_call_target="tpu_custom_call" | custom-call | flops 2147483648 | bytes 15204352 | tf_op jit(solution)/shard_map/pallas_call | solution.py:99
  103.4 2.5 %collective-permute-start.17 = (bf16[64,1024]{1,0:T(8,128)(2,1)S(1)}, bf16[64,1024]{1,0:T(8,128)(2,1)S(1)}, u32[]{:S(2)}, u32[]{:S(2)}) collective-permute-start(bf16[64,1024]{1,0:T(8,128)(2,1)S(1)} %get-tuple-element.81), channel_id=1, source_target_pairs={{0,20},{4,16},{8,28},{12,24},{16,4},{20,0},{24,12},{28,8},{1,21},{... | collective-permute-start | bytes 393224 | tf_op jit(solution)/shard_map/ppermute | solution.py:390
  106.9 2.7 %shard_map.77.refs_0_ = bf16[256,1024]{1,0:T(8,128)(2,1)S(1)} custom-call(bf16[64,1024]{1,0:T(8,128)(2,1)S(1)} %collective-permute-done.13.refs_0_, bf16[64,1024]{1,0:T(8,128)(2,1)S(1)} %collective-permute-done.14.refs_1_, bf16[64,1024]{1,0:T(8,128)(2,1)S(1)} %collective-permute-done.15.refs_2_, bf16[64,1024]{1,0:T(8,128)(2,1)S(1)} %collective-permute-done.16.refs_3_, ...), custom_call_target="tpu_custom_call" | custom-call | flops 2147483648 | bytes 9437184 | tf_op jit(solution)/shard_map/pallas_call | solution.py:99
  (33 shorter events, 14.0 us)
Async XLA Ops:
  3.4 21.9 %copy-start = (bf16[1024,3072]{1,0:T(8,128)(2,1)}, bf16[1024,3072]{1,0:T(8,128)(2,1)S(1)}, u32[]{:S(2)}) copy-start(bf16[1024,3072]{1,0:T(8,128)(2,1)S(1)} %get-tuple-element.51.refs_4_) | copy-start | bytes 18874372
  5.2 8.2 %collective-permute-start.10 = (bf16[64,1024]{1,0:T(8,128)(2,1)S(1)}, bf16[64,1024]{1,0:T(8,128)(2,1)S(1)}, u32[]{:S(2)}, u32[]{:S(2)}) collective-permute-start(bf16[64,1024]{1,0:T(8,128)(2,1)S(1)} %bitcast.18), channel_id=1, source_target_pairs={{0,1},{1,0},{2,3},{3,2},{4,5},{5,4},{6,7},{7,6},{8,9},{9,8},{10,11... | collective-permute-start | bytes 393224 | tf_op jit(solution)/shard_map/ppermute | solution.py:390
  8.4 12.9 %collective-permute-start.11 = (bf16[64,1024]{1,0:T(8,128)(2,1)S(1)}, bf16[64,1024]{1,0:T(8,128)(2,1)S(1)}, u32[]{:S(2)}, u32[]{:S(2)}) collective-permute-start(bf16[64,1024]{1,0:T(8,128)(2,1)S(1)} %bitcast.16), channel_id=1, source_target_pairs={{0,2},{1,3},{2,0},{3,1},{4,6},{5,7},{6,4},{7,5},{8,10},{9,11},{10,... | collective-permute-start | bytes 393224 | tf_op jit(solution)/shard_map/ppermute | solution.py:390
  10.9 10.3 %collective-permute-start.12 = (bf16[64,1024]{1,0:T(8,128)(2,1)S(1)}, bf16[64,1024]{1,0:T(8,128)(2,1)S(1)}, u32[]{:S(2)}, u32[]{:S(2)}) collective-permute-start(bf16[64,1024]{1,0:T(8,128)(2,1)S(1)} %bitcast.14), channel_id=1, source_target_pairs={{0,3},{1,2},{2,1},{3,0},{4,7},{5,6},{6,5},{7,4},{8,11},{9,10},{10,... | collective-permute-start | bytes 393224 | tf_op jit(solution)/shard_map/ppermute | solution.py:390
  25.4 61.9 %all-to-all-start = ((bf16[32,8,1024]{2,1,0:T(8,128)(2,1)}), bf16[32,8,1024]{2,1,0:T(8,128)(2,1)S(1)}, u32[]{:S(2)}, u32[]{:S(2)}) async-start(bf16[32,8,1024]{2,1,0:T(8,128)(2,1)} %bitcast.8), calls=%async_computation | async-start | bytes 1048576 | tf_op jit(solution)/shard_map/all_to_all | solution.py:467
  32.0 12.0 %collective-permute-start = (bf16[64,1024]{1,0:T(8,128)(2,1)S(1)}, bf16[64,1024]{1,0:T(8,128)(2,1)S(1)}, u32[]{:S(2)}, u32[]{:S(2)}) collective-permute-start(bf16[64,1024]{1,0:T(8,128)(2,1)S(1)} %bitcast.19), channel_id=1, source_target_pairs={{0,1},{1,0},{2,3},{3,2},{4,5},{5,4},{6,7},{7,6},{8,9},{9,8},{10,11... | collective-permute-start | bytes 393224 | tf_op jit(solution)/shard_map/ppermute | solution.py:390
  33.8 20.8 %collective-permute-start.1 = (bf16[64,1024]{1,0:T(8,128)(2,1)S(1)}, bf16[64,1024]{1,0:T(8,128)(2,1)S(1)}, u32[]{:S(2)}, u32[]{:S(2)}) collective-permute-start(bf16[64,1024]{1,0:T(8,128)(2,1)S(1)} %bitcast.17), channel_id=1, source_target_pairs={{0,2},{1,3},{2,0},{3,1},{4,6},{5,7},{6,4},{7,5},{8,10},{9,11},{10,... | collective-permute-start | bytes 393224 | tf_op jit(solution)/shard_map/ppermute | solution.py:390
  36.2 18.4 %collective-permute-start.2 = (bf16[64,1024]{1,0:T(8,128)(2,1)S(1)}, bf16[64,1024]{1,0:T(8,128)(2,1)S(1)}, u32[]{:S(2)}, u32[]{:S(2)}) collective-permute-start(bf16[64,1024]{1,0:T(8,128)(2,1)S(1)} %bitcast.15), channel_id=1, source_target_pairs={{0,3},{1,2},{2,1},{3,0},{4,7},{5,6},{6,5},{7,4},{8,11},{9,10},{10,... | collective-permute-start | bytes 393224 | tf_op jit(solution)/shard_map/ppermute | solution.py:390
  54.6 2.8 %copy-start.1 = (bf16[1024,3072]{1,0:T(8,128)(2,1)S(1)}, bf16[1024,3072]{1,0:T(8,128)(2,1)}, u32[]{:S(2)}) copy-start(bf16[1024,3072]{1,0:T(8,128)(2,1)} %copy-done) | copy-start | bytes 18874372
  60.7 7.4 %collective-permute-start.3 = (bf16[64,1024]{1,0:T(8,128)(2,1)S(1)}, bf16[64,1024]{1,0:T(8,128)(2,1)S(1)}, u32[]{:S(2)}, u32[]{:S(2)}) collective-permute-start(bf16[64,1024]{1,0:T(8,128)(2,1)S(1)} %get-tuple-element.54), channel_id=1, source_target_pairs={{0,1},{1,0},{2,3},{3,2},{4,5},{5,4},{6,7},{7,6},{8,9},{9,8},{10,11... | collective-permute-start | bytes 393224 | tf_op jit(solution)/shard_map/ppermute | solution.py:390
  63.6 12.5 %collective-permute-start.4 = (bf16[64,1024]{1,0:T(8,128)(2,1)S(1)}, bf16[64,1024]{1,0:T(8,128)(2,1)S(1)}, u32[]{:S(2)}, u32[]{:S(2)}) collective-permute-start(bf16[64,1024]{1,0:T(8,128)(2,1)S(1)} %get-tuple-element.55), channel_id=1, source_target_pairs={{0,2},{1,3},{2,0},{3,1},{4,6},{5,7},{6,4},{7,5},{8,10},{9,11},{10,... | collective-permute-start | bytes 393224 | tf_op jit(solution)/shard_map/ppermute | solution.py:390
  63.7 12.5 %collective-permute-start.5 = (bf16[64,1024]{1,0:T(8,128)(2,1)S(1)}, bf16[64,1024]{1,0:T(8,128)(2,1)S(1)}, u32[]{:S(2)}, u32[]{:S(2)}) collective-permute-start(bf16[64,1024]{1,0:T(8,128)(2,1)S(1)} %get-tuple-element.56), channel_id=1, source_target_pairs={{0,3},{1,2},{2,1},{3,0},{4,7},{5,6},{6,5},{7,4},{8,11},{9,10},{10,... | collective-permute-start | bytes 393224 | tf_op jit(solution)/shard_map/ppermute | solution.py:390
  76.2 1.6 %collective-permute-start.6 = (bf16[128,1024]{1,0:T(8,128)(2,1)S(1)}, bf16[128,1024]{1,0:T(8,128)(2,1)S(1)}, u32[]{:S(2)}, u32[]{:S(2)}) collective-permute-start(bf16[128,1024]{1,0:T(8,128)(2,1)S(1)} %shard_map.74), channel_id=1, source_target_pairs={{0,4},{4,0},{8,12},{12,8},{16,20},{20,16},{24,28},{28,24},{1,5},{5... | collective-permute-start | bytes 786440 | tf_op jit(solution)/shard_map/ppermute | solution.py:390
  77.8 6.2 %collective-permute-start.7 = (bf16[64,1024]{1,0:T(8,128)(2,1)S(1)}, bf16[64,1024]{1,0:T(8,128)(2,1)S(1)}, u32[]{:S(2)}, u32[]{:S(2)}) collective-permute-start(bf16[64,1024]{1,0:T(8,128)(2,1)S(1)} %get-tuple-element.58), channel_id=1, source_target_pairs={{0,8},{4,12},{8,0},{12,4},{16,24},{20,28},{24,16},{28,20},{1,9},{5... | collective-permute-start | bytes 393224 | tf_op jit(solution)/shard_map/ppermute | solution.py:429
  79.2 8.1 %collective-permute-start.8 = (bf16[64,1024]{1,0:T(8,128)(2,1)S(1)}, bf16[64,1024]{1,0:T(8,128)(2,1)S(1)}, u32[]{:S(2)}, u32[]{:S(2)}) collective-permute-start(bf16[64,1024]{1,0:T(8,128)(2,1)S(1)} %get-tuple-element.59), channel_id=1, source_target_pairs={{0,16},{4,20},{8,24},{12,28},{16,0},{20,4},{24,8},{28,12},{1,17},{... | collective-permute-start | bytes 393224 | tf_op jit(solution)/shard_map/ppermute | solution.py:429
  80.7 6.6 %collective-permute-start.9 = (bf16[64,1024]{1,0:T(8,128)(2,1)S(1)}, bf16[64,1024]{1,0:T(8,128)(2,1)S(1)}, u32[]{:S(2)}, u32[]{:S(2)}) collective-permute-start(bf16[64,1024]{1,0:T(8,128)(2,1)S(1)} %get-tuple-element.60), channel_id=1, source_target_pairs={{0,24},{4,28},{8,16},{12,20},{16,8},{20,12},{24,0},{28,4},{1,25},{... | collective-permute-start | bytes 393224 | tf_op jit(solution)/shard_map/ppermute | solution.py:429
  95.4 10.5 %collective-permute-start.13 = (bf16[64,1024]{1,0:T(8,128)(2,1)S(1)}, bf16[64,1024]{1,0:T(8,128)(2,1)S(1)}, u32[]{:S(2)}, u32[]{:S(2)}) collective-permute-start(bf16[64,1024]{1,0:T(8,128)(2,1)S(1)} %get-tuple-element.66), channel_id=1, source_target_pairs={{0,8},{4,12},{8,0},{12,4},{16,24},{20,28},{24,16},{28,20},{1,9},{5... | collective-permute-start | bytes 393224 | tf_op jit(solution)/shard_map/ppermute | solution.py:390
  96.6 10.0 %collective-permute-start.14 = (bf16[64,1024]{1,0:T(8,128)(2,1)S(1)}, bf16[64,1024]{1,0:T(8,128)(2,1)S(1)}, u32[]{:S(2)}, u32[]{:S(2)}) collective-permute-start(bf16[64,1024]{1,0:T(8,128)(2,1)S(1)} %get-tuple-element.67), channel_id=1, source_target_pairs={{0,16},{4,20},{8,24},{12,28},{16,0},{20,4},{24,8},{28,12},{1,17},{... | collective-permute-start | bytes 393224 | tf_op jit(solution)/shard_map/ppermute | solution.py:390
  97.5 9.4 %collective-permute-start.15 = (bf16[64,1024]{1,0:T(8,128)(2,1)S(1)}, bf16[64,1024]{1,0:T(8,128)(2,1)S(1)}, u32[]{:S(2)}, u32[]{:S(2)}) collective-permute-start(bf16[64,1024]{1,0:T(8,128)(2,1)S(1)} %get-tuple-element.68), channel_id=1, source_target_pairs={{0,24},{4,28},{8,16},{12,20},{16,8},{20,12},{24,0},{28,4},{1,25},{... | collective-permute-start | bytes 393224 | tf_op jit(solution)/shard_map/ppermute | solution.py:390
  98.9 7.9 %collective-permute-start.16 = (bf16[64,1024]{1,0:T(8,128)(2,1)S(1)}, bf16[64,1024]{1,0:T(8,128)(2,1)S(1)}, u32[]{:S(2)}, u32[]{:S(2)}) collective-permute-start(bf16[64,1024]{1,0:T(8,128)(2,1)S(1)} %get-tuple-element.69), channel_id=1, source_target_pairs={{0,28},{4,24},{8,20},{12,16},{16,12},{20,8},{24,4},{28,0},{1,29},{... | collective-permute-start | bytes 393224 | tf_op jit(solution)/shard_map/ppermute | solution.py:390
  103.4 6.1 %collective-permute-start.17 = (bf16[64,1024]{1,0:T(8,128)(2,1)S(1)}, bf16[64,1024]{1,0:T(8,128)(2,1)S(1)}, u32[]{:S(2)}, u32[]{:S(2)}) collective-permute-start(bf16[64,1024]{1,0:T(8,128)(2,1)S(1)} %get-tuple-element.81), channel_id=1, source_target_pairs={{0,20},{4,16},{8,28},{12,24},{16,4},{20,0},{24,12},{28,8},{1,21},{... | collective-permute-start | bytes 393224 | tf_op jit(solution)/shard_map/ppermute | solution.py:390
  105.9 5.3 %collective-permute-start.18 = (bf16[64,1024]{1,0:T(8,128)(2,1)S(1)}, bf16[64,1024]{1,0:T(8,128)(2,1)S(1)}, u32[]{:S(2)}, u32[]{:S(2)}) collective-permute-start(bf16[64,1024]{1,0:T(8,128)(2,1)S(1)} %get-tuple-element.82), channel_id=1, source_target_pairs={{0,12},{4,8},{8,4},{12,0},{16,28},{20,24},{24,20},{28,16},{1,13},{... | collective-permute-start | bytes 393224 | tf_op jit(solution)/shard_map/ppermute | solution.py:390
  106.7 4.5 %collective-permute-start.19 = (bf16[64,1024]{1,0:T(8,128)(2,1)S(1)}, bf16[64,1024]{1,0:T(8,128)(2,1)S(1)}, u32[]{:S(2)}, u32[]{:S(2)}) collective-permute-start(bf16[64,1024]{1,0:T(8,128)(2,1)S(1)} %get-tuple-element.83), channel_id=1, source_target_pairs={{0,4},{4,0},{8,12},{12,8},{16,20},{20,16},{24,28},{28,24},{1,5},{5... | collective-permute-start | bytes 393224 | tf_op jit(solution)/shard_map/ppermute | solution.py:390

commit v3 on v2

--- a/solution.py
+++ b/solution.py
@@ -11,7 +11,7 @@
 
 HEADS = 8
 CHUNKS = 2
-PIECES = 4
+PIECES = 2
 BF = jnp.bfloat16
 F32 = jnp.float32
 
@@ -438,7 +438,7 @@
     chips = nr // 2
     cell = rows * cpd
     g = dict(nr=nr, nc=nc, rows=rows, cols=cols, cpd=cpd, span=8)
-    z_order = list(range(nc - 1, 0, -1))
+    z_order = col_order(nc)
 
     def enter(t, latents):
         slots = split(latents, nc, band, t * rows, rows)
@@ -482,12 +482,16 @@
     return out.reshape(local_rows, cols, width)
 
 
+def col_order(nc):
+    return sorted(range(1, nc), key=lambda k: (bin(k).count("1"), -k))
+
+
 def chip_order(nr):
     return sorted(range(1, nr // 2), key=lambda q: bin(q).count("1"))
 
 
 def groups(nr):
-    near = sorted([*range(2, nr, 2), nr - 1], key=lambda m: bin(m // 2).count("1"))
+    near = sorted([*range(2, nr, 2), nr - 1], key=lambda m: (-bin(m // 2).count("1"), m))
     return near, [m for m in range(nr - 1, -1, -1) if m not in near]
 
 

time: 113 us -> 112 us (level)
  no operation moved by 1% of the time
where the time goes in v3:
time: 112 us
  waiting for transfers between devices  48.2 us (43%)
  starting transfers between devices  30.9 us (28%)
  Pallas kernels  29.5 us (26%)
  local copies, waits for them, and re-layouts  2.79 us (2%)
    ppermute x17, waiting for transfers between devices, swap(): lax.ppermute(x, axis, [(i, i ^ k) for i in range(size)])  42.2 us
    ppermute x17, starting transfers between devices, swap(): lax.ppermute(x, axis, [(i, i ^ k) for i in range(size)])  21.9 us
    pallas_call x6, Pallas kernels, call(): pl.pallas_call(kernel, in_specs=[VMEM_SPEC] * len(ins), out_specs=[VMEM_S...  14.7 us
    pallas_call x1, Pallas kernels, finish_stage(): pl.pallas_call(functools.partial(finish_kernel, g, members, [len(part) fo...  7.26 us
    ppermute x3, waiting for transfers between devices, spread(): lax.ppermute(parts[q], 'row', [(i, i ^ 2 * q) for i in range(2 * n)])  5.93 us
    all_to_all x1, starting transfers between devices, on_device(): lax.all_to_all(parts, ('row', 'col'), split_axis=0, concat_axis=0, tiled=...  5.43 us
    ppermute x3, starting transfers between devices, spread(): lax.ppermute(parts[q], 'row', [(i, i ^ 2 * q) for i in range(2 * n)])  3.55 us
    pallas_call x1, Pallas kernels, fetch(): pl.pallas_call(functools.partial(fetch_kernel, count, pieces), in_specs=[...  3.43 us
  transfers between devices with their start and end apart: 21, of which 11 were waited for; matrix products, arithmetic and copies ran while one was open for 0% of the time, Pallas kernels for 10%

profile of v3, /device:TPU:0, one launch (start us, length us, event | category | flops | bytes accessed | tf_op | source)
XLA Modules:
  0.0 111.7 jit_solution(13961972989559409928)
XLA Ops:
  0.0 3.4 %fetch.1 = (bf16[1024,3072]{1,0:T(8,128)(2,1)S(1)}, bf16[1024,1024]{1,0:T(8,128)(2,1)S(1)}) custom-call(bf16[1024,3072]{1,0:T(8,128)(2,1)} %refs_0_.1, bf16[1024,1024]{1,0:T(8,128)(2,1)} %refs_1_.1), custom_call_target="tpu_custom_call" | custom-call | bytes 16777216 | tf_op jit(solution)/shard_map/fetch/pallas_call | solution.py:154
  3.4 1.8 %split.3 = (bf16[4,16,1024]{2,1,0:T(8,128)(2,1)S(1)}, bf16[4,16,1024]{2,1,0:T(8,128)(2,1)S(1)}, bf16[4,16,1024]{2,1,0:T(8,128)(2,1)S(1)}, bf16[4,16,1024]{2,1,0:T(8,128)(2,1)S(1)}) custom-call(bf16[32,16,1024]{2,1,0:T(8,128)(2,1)} %latents.2), custom_call_target="tpu_custom_call" | custom-call | bytes 1048576 | tf_op jit(solution)/shard_map/split/pallas_call | solution.py:125
  5.2 3.1 %collective-permute-start.10 = (bf16[64,1024]{1,0:T(8,128)(2,1)S(1)}, bf16[64,1024]{1,0:T(8,128)(2,1)S(1)}, u32[]{:S(2)}, u32[]{:S(2)}) collective-permute-start(bf16[64,1024]{1,0:T(8,128)(2,1)S(1)} %bitcast.18), channel_id=1, source_target_pairs={{0,1},{1,0},{2,3},{3,2},{4,5},{5,4},{6,7},{7,6},{8,9},{9,8},{10,11... | collective-permute-start | bytes 393224 | tf_op jit(solution)/shard_map/ppermute | solution.py:390
  8.4 2.6 %collective-permute-start.11 = (bf16[64,1024]{1,0:T(8,128)(2,1)S(1)}, bf16[64,1024]{1,0:T(8,128)(2,1)S(1)}, u32[]{:S(2)}, u32[]{:S(2)}) collective-permute-start(bf16[64,1024]{1,0:T(8,128)(2,1)S(1)} %bitcast.16), channel_id=1, source_target_pairs={{0,2},{1,3},{2,0},{3,1},{4,6},{5,7},{6,4},{7,5},{8,10},{9,11},{10,... | collective-permute-start | bytes 393224 | tf_op jit(solution)/shard_map/ppermute | solution.py:390
  10.9 2.5 %collective-permute-done.10.refs_1_ = bf16[64,1024]{1,0:T(8,128)(2,1)S(1)} collective-permute-done((bf16[64,1024]{1,0:T(8,128)(2,1)S(1)}, bf16[64,1024]{1,0:T(8,128)(2,1)S(1)}, u32[]{:S(2)}, u32[]{:S(2)}) %collective-permute-start.10) | collective-permute-done | bytes 131104 | tf_op jit(solution)/shard_map/ppermute | solution.py:390
  13.4 7.8 %collective-permute-done.11.refs_2_ = bf16[64,1024]{1,0:T(8,128)(2,1)S(1)} collective-permute-done((bf16[64,1024]{1,0:T(8,128)(2,1)S(1)}, bf16[64,1024]{1,0:T(8,128)(2,1)S(1)}, u32[]{:S(2)}, u32[]{:S(2)}) %collective-permute-start.11) | collective-permute-done | bytes 131104 | tf_op jit(solution)/shard_map/ppermute | solution.py:390
  21.2 4.1 %shard_map.76 = bf16[256,1024]{1,0:T(8,128)(2,1)} custom-call(bf16[64,1024]{1,0:T(8,128)(2,1)S(1)} %bitcast.13, bf16[64,1024]{1,0:T(8,128)(2,1)S(1)} %collective-permute-done.10.refs_1_, bf16[64,1024]{1,0:T(8,128)(2,1)S(1)} %collective-permute-done.11.refs_2_, bf16[64,1024]{1,0:T(8,128)(2,1)S(1)} %collective-permute-done.12.refs_3_, ...), custom_call_target="tpu_custom_call" | custom-call | flops 2147483648 | bytes 9437184 | tf_op jit(solution)/shard_map/pallas_call | solution.py:99
  25.4 5.4 %all-to-all-start = ((bf16[32,8,1024]{2,1,0:T(8,128)(2,1)}), bf16[32,8,1024]{2,1,0:T(8,128)(2,1)S(1)}, u32[]{:S(2)}, u32[]{:S(2)}) async-start(bf16[32,8,1024]{2,1,0:T(8,128)(2,1)} %bitcast.8), calls=%async_computation | async-start | bytes 1048576 | tf_op jit(solution)/shard_map/all_to_all | solution.py:467
  32.0 1.8 %collective-permute-start = (bf16[64,1024]{1,0:T(8,128)(2,1)S(1)}, bf16[64,1024]{1,0:T(8,128)(2,1)S(1)}, u32[]{:S(2)}, u32[]{:S(2)}) collective-permute-start(bf16[64,1024]{1,0:T(8,128)(2,1)S(1)} %bitcast.19), channel_id=1, source_target_pairs={{0,1},{1,0},{2,3},{3,2},{4,5},{5,4},{6,7},{7,6},{8,9},{9,8},{10,11... | collective-permute-start | bytes 393224 | tf_op jit(solution)/shard_map/ppermute | solution.py:390
  33.8 2.4 %collective-permute-start.1 = (bf16[64,1024]{1,0:T(8,128)(2,1)S(1)}, bf16[64,1024]{1,0:T(8,128)(2,1)S(1)}, u32[]{:S(2)}, u32[]{:S(2)}) collective-permute-start(bf16[64,1024]{1,0:T(8,128)(2,1)S(1)} %bitcast.17), channel_id=1, source_target_pairs={{0,2},{1,3},{2,0},{3,1},{4,6},{5,7},{6,4},{7,5},{8,10},{9,11},{10,... | collective-permute-start | bytes 393224 | tf_op jit(solution)/shard_map/ppermute | solution.py:390
  36.4 7.6 %collective-permute-done.refs_1_ = bf16[64,1024]{1,0:T(8,128)(2,1)S(1)} collective-permute-done((bf16[64,1024]{1,0:T(8,128)(2,1)S(1)}, bf16[64,1024]{1,0:T(8,128)(2,1)S(1)}, u32[]{:S(2)}, u32[]{:S(2)}) %collective-permute-start) | collective-permute-done | bytes 131104 | tf_op jit(solution)/shard_map/ppermute | solution.py:390
  44.0 10.6 %collective-permute-done.1.refs_2_ = bf16[64,1024]{1,0:T(8,128)(2,1)S(1)} collective-permute-done((bf16[64,1024]{1,0:T(8,128)(2,1)S(1)}, bf16[64,1024]{1,0:T(8,128)(2,1)S(1)}, u32[]{:S(2)}, u32[]{:S(2)}) %collective-permute-start.1) | collective-permute-done | bytes 131104 | tf_op jit(solution)/shard_map/ppermute | solution.py:390
  54.6 2.8 %copy-done.1 = bf16[1024,3072]{1,0:T(8,128)(2,1)S(1)} copy-done((bf16[1024,3072]{1,0:T(8,128)(2,1)S(1)}, bf16[1024,3072]{1,0:T(8,128)(2,1)}, u32[]{:S(2)}) %copy-start.1) | copy-done | bytes 6291480
  57.4 3.3 %shard_map.73 = (bf16[64,1024]{1,0:T(8,128)(2,1)S(1)}, bf16[64,1024]{1,0:T(8,128)(2,1)S(1)}, bf16[64,1024]{1,0:T(8,128)(2,1)S(1)}, bf16[64,1024]{1,0:T(8,128)(2,1)S(1)}) custom-call(bf16[64,1024]{1,0:T(8,128)(2,1)S(1)} %bitcast.12, bf16[64,1024]{1,0:T(8,128)(2,1)S(1)} %collective-permute-done.refs_1_, bf16[64,1024]{1,0:T(8,128)(2,1)S(1)} %collective-permute-done.1.refs_2_, ...), custom_call_target="tpu_custom_call" | custom-call | flops 2147483648 | bytes 9437184 | tf_op jit(solution)/shard_map/pallas_call | solution.py:99
  60.7 2.9 %collective-permute-start.3 = (bf16[64,1024]{1,0:T(8,128)(2,1)S(1)}, bf16[64,1024]{1,0:T(8,128)(2,1)S(1)}, u32[]{:S(2)}, u32[]{:S(2)}) collective-permute-start(bf16[64,1024]{1,0:T(8,128)(2,1)S(1)} %get-tuple-element.54), channel_id=1, source_target_pairs={{0,1},{1,0},{2,3},{3,2},{4,5},{5,4},{6,7},{7,6},{8,9},{9,8},{10,11... | collective-permute-start | bytes 393224 | tf_op jit(solution)/shard_map/ppermute | solution.py:390
  63.7 2.4 %collective-permute-start.5 = (bf16[64,1024]{1,0:T(8,128)(2,1)S(1)}, bf16[64,1024]{1,0:T(8,128)(2,1)S(1)}, u32[]{:S(2)}, u32[]{:S(2)}) collective-permute-start(bf16[64,1024]{1,0:T(8,128)(2,1)S(1)} %get-tuple-element.56), channel_id=1, source_target_pairs={{0,3},{1,2},{2,1},{3,0},{4,7},{5,6},{6,5},{7,4},{8,11},{9,10},{10,... | collective-permute-start | bytes 393224 | tf_op jit(solution)/shard_map/ppermute | solution.py:390
  66.0 2.1 %collective-permute-done.3.refs_1_ = bf16[64,1024]{1,0:T(8,128)(2,1)S(1)} collective-permute-done((bf16[64,1024]{1,0:T(8,128)(2,1)S(1)}, bf16[64,1024]{1,0:T(8,128)(2,1)S(1)}, u32[]{:S(2)}, u32[]{:S(2)}) %collective-permute-start.3) | collective-permute-done | bytes 131104 | tf_op jit(solution)/shard_map/ppermute | solution.py:390
  68.2 8.0 %collective-permute-done.4.refs_2_ = bf16[64,1024]{1,0:T(8,128)(2,1)S(1)} collective-permute-done((bf16[64,1024]{1,0:T(8,128)(2,1)S(1)}, bf16[64,1024]{1,0:T(8,128)(2,1)S(1)}, u32[]{:S(2)}, u32[]{:S(2)}) %collective-permute-start.4) | collective-permute-done | bytes 131104 | tf_op jit(solution)/shard_map/ppermute | solution.py:390
  81.3 2.6 %collective-permute-done.7.refs_1_ = bf16[64,1024]{1,0:T(8,128)(2,1)S(1)} collective-permute-done((bf16[64,1024]{1,0:T(8,128)(2,1)S(1)}, bf16[64,1024]{1,0:T(8,128)(2,1)S(1)}, u32[]{:S(2)}, u32[]{:S(2)}) %collective-permute-start.7) | collective-permute-done | bytes 131104 | tf_op jit(solution)/shard_map/ppermute | solution.py:429
  84.0 3.3 %collective-permute-done.8.refs_2_ = bf16[64,1024]{1,0:T(8,128)(2,1)S(1)} collective-permute-done((bf16[64,1024]{1,0:T(8,128)(2,1)S(1)}, bf16[64,1024]{1,0:T(8,128)(2,1)S(1)}, u32[]{:S(2)}, u32[]{:S(2)}) %collective-permute-start.8) | collective-permute-done | bytes 131104 | tf_op jit(solution)/shard_map/ppermute | solution.py:429
  87.3 7.3 %finish_stage.1 = (bf16[256,1024]{1,0:T(8,128)(2,1)S(1)}, bf16[256,1024]{1,0:T(8,128)(2,1)S(1)}, bf16[256,1024]{1,0:T(8,128)(2,1)S(1)}, bf16[256,1024]{1,0:T(8,1...) custom-call(bf16[64,1024]{1,0:T(8,128)(2,1)S(1)} %get-tuple-element., ...), custom_call_target="tpu_custom_call" | custom-call | flops 4294967296 | bytes 16777216 | tf_op jit(solution)/shard_map/finish_stage/pallas_call | solution.py:303
  98.1 4.5 %shard_map.78 = (bf16[64,1024]{1,0:T(8,128)(2,1)S(1)}, bf16[64,1024]{1,0:T(8,128)(2,1)S(1)}, bf16[64,1024]{1,0:T(8,128)(2,1)S(1)}, bf16[64,1024]{1,0:T(8,128)(2,1)S(1)}) custom-call(bf16[256,1024]{1,0:T(8,128)(2,1)S(1)} %get-tuple-element.72.refs_0_, bf16[256,1024]{1,0:T(8,128)(2,1)S(1)} %get-tuple-element.73.refs_1_, ...), custom_call_target="tpu_custom_call" | custom-call | flops 2147483648 | bytes 15204352 | tf_op jit(solution)/shard_map/pallas_call | solution.py:99
  102.6 1.9 %collective-permute-start.17 = (bf16[64,1024]{1,0:T(8,128)(2,1)S(1)}, bf16[64,1024]{1,0:T(8,128)(2,1)S(1)}, u32[]{:S(2)}, u32[]{:S(2)}) collective-permute-start(bf16[64,1024]{1,0:T(8,128)(2,1)S(1)} %get-tuple-element.81), channel_id=1, source_target_pairs={{0,20},{4,16},{8,28},{12,24},{16,4},{20,0},{24,12},{28,8},{1,21},{... | collective-permute-start | bytes 393224 | tf_op jit(solution)/shard_map/ppermute | solution.py:390
  106.2 2.7 %shard_map.77.refs_0_ = bf16[256,1024]{1,0:T(8,128)(2,1)S(1)} custom-call(bf16[64,1024]{1,0:T(8,128)(2,1)S(1)} %collective-permute-done.13.refs_0_, bf16[64,1024]{1,0:T(8,128)(2,1)S(1)} %collective-permute-done.14.refs_1_, bf16[64,1024]{1,0:T(8,128)(2,1)S(1)} %collective-permute-done.15.refs_2_, bf16[64,1024]{1,0:T(8,128)(2,1)S(1)} %collective-permute-done.16.refs_3_, ...), custom_call_target="tpu_custom_call" | custom-call | flops 2147483648 | bytes 9437184 | tf_op jit(solution)/shard_map/pallas_call | solution.py:99
  (33 shorter events, 14.5 us)
Async XLA Ops:
  3.4 21.9 %copy-start = (bf16[1024,3072]{1,0:T(8,128)(2,1)}, bf16[1024,3072]{1,0:T(8,128)(2,1)S(1)}, u32[]{:S(2)}) copy-start(bf16[1024,3072]{1,0:T(8,128)(2,1)S(1)} %get-tuple-element.51.refs_4_) | copy-start | bytes 18874372
  5.2 8.2 %collective-permute-start.10 = (bf16[64,1024]{1,0:T(8,128)(2,1)S(1)}, bf16[64,1024]{1,0:T(8,128)(2,1)S(1)}, u32[]{:S(2)}, u32[]{:S(2)}) collective-permute-start(bf16[64,1024]{1,0:T(8,128)(2,1)S(1)} %bitcast.18), channel_id=1, source_target_pairs={{0,1},{1,0},{2,3},{3,2},{4,5},{5,4},{6,7},{7,6},{8,9},{9,8},{10,11... | collective-permute-start | bytes 393224 | tf_op jit(solution)/shard_map/ppermute | solution.py:390
  8.4 12.9 %collective-permute-start.11 = (bf16[64,1024]{1,0:T(8,128)(2,1)S(1)}, bf16[64,1024]{1,0:T(8,128)(2,1)S(1)}, u32[]{:S(2)}, u32[]{:S(2)}) collective-permute-start(bf16[64,1024]{1,0:T(8,128)(2,1)S(1)} %bitcast.16), channel_id=1, source_target_pairs={{0,2},{1,3},{2,0},{3,1},{4,6},{5,7},{6,4},{7,5},{8,10},{9,11},{10,... | collective-permute-start | bytes 393224 | tf_op jit(solution)/shard_map/ppermute | solution.py:390
  10.9 10.3 %collective-permute-start.12 = (bf16[64,1024]{1,0:T(8,128)(2,1)S(1)}, bf16[64,1024]{1,0:T(8,128)(2,1)S(1)}, u32[]{:S(2)}, u32[]{:S(2)}) collective-permute-start(bf16[64,1024]{1,0:T(8,128)(2,1)S(1)} %bitcast.14), channel_id=1, source_target_pairs={{0,3},{1,2},{2,1},{3,0},{4,7},{5,6},{6,5},{7,4},{8,11},{9,10},{10,... | collective-permute-start | bytes 393224 | tf_op jit(solution)/shard_map/ppermute | solution.py:390
  25.4 61.9 %all-to-all-start = ((bf16[32,8,1024]{2,1,0:T(8,128)(2,1)}), bf16[32,8,1024]{2,1,0:T(8,128)(2,1)S(1)}, u32[]{:S(2)}, u32[]{:S(2)}) async-start(bf16[32,8,1024]{2,1,0:T(8,128)(2,1)} %bitcast.8), calls=%async_computation | async-start | bytes 1048576 | tf_op jit(solution)/shard_map/all_to_all | solution.py:467
  32.0 12.0 %collective-permute-start = (bf16[64,1024]{1,0:T(8,128)(2,1)S(1)}, bf16[64,1024]{1,0:T(8,128)(2,1)S(1)}, u32[]{:S(2)}, u32[]{:S(2)}) collective-permute-start(bf16[64,1024]{1,0:T(8,128)(2,1)S(1)} %bitcast.19), channel_id=1, source_target_pairs={{0,1},{1,0},{2,3},{3,2},{4,5},{5,4},{6,7},{7,6},{8,9},{9,8},{10,11... | collective-permute-start | bytes 393224 | tf_op jit(solution)/shard_map/ppermute | solution.py:390
  33.8 20.8 %collective-permute-start.1 = (bf16[64,1024]{1,0:T(8,128)(2,1)S(1)}, bf16[64,1024]{1,0:T(8,128)(2,1)S(1)}, u32[]{:S(2)}, u32[]{:S(2)}) collective-permute-start(bf16[64,1024]{1,0:T(8,128)(2,1)S(1)} %bitcast.17), channel_id=1, source_target_pairs={{0,2},{1,3},{2,0},{3,1},{4,6},{5,7},{6,4},{7,5},{8,10},{9,11},{10,... | collective-permute-start | bytes 393224 | tf_op jit(solution)/shard_map/ppermute | solution.py:390
  36.2 18.4 %collective-permute-start.2 = (bf16[64,1024]{1,0:T(8,128)(2,1)S(1)}, bf16[64,1024]{1,0:T(8,128)(2,1)S(1)}, u32[]{:S(2)}, u32[]{:S(2)}) collective-permute-start(bf16[64,1024]{1,0:T(8,128)(2,1)S(1)} %bitcast.15), channel_id=1, source_target_pairs={{0,3},{1,2},{2,1},{3,0},{4,7},{5,6},{6,5},{7,4},{8,11},{9,10},{10,... | collective-permute-start | bytes 393224 | tf_op jit(solution)/shard_map/ppermute | solution.py:390
  54.6 2.8 %copy-start.1 = (bf16[1024,3072]{1,0:T(8,128)(2,1)S(1)}, bf16[1024,3072]{1,0:T(8,128)(2,1)}, u32[]{:S(2)}) copy-start(bf16[1024,3072]{1,0:T(8,128)(2,1)} %copy-done) | copy-start | bytes 18874372
  60.7 7.4 %collective-permute-start.3 = (bf16[64,1024]{1,0:T(8,128)(2,1)S(1)}, bf16[64,1024]{1,0:T(8,128)(2,1)S(1)}, u32[]{:S(2)}, u32[]{:S(2)}) collective-permute-start(bf16[64,1024]{1,0:T(8,128)(2,1)S(1)} %get-tuple-element.54), channel_id=1, source_target_pairs={{0,1},{1,0},{2,3},{3,2},{4,5},{5,4},{6,7},{7,6},{8,9},{9,8},{10,11... | collective-permute-start | bytes 393224 | tf_op jit(solution)/shard_map/ppermute | solution.py:390
  63.6 12.5 %collective-permute-start.4 = (bf16[64,1024]{1,0:T(8,128)(2,1)S(1)}, bf16[64,1024]{1,0:T(8,128)(2,1)S(1)}, u32[]{:S(2)}, u32[]{:S(2)}) collective-permute-start(bf16[64,1024]{1,0:T(8,128)(2,1)S(1)} %get-tuple-element.55), channel_id=1, source_target_pairs={{0,2},{1,3},{2,0},{3,1},{4,6},{5,7},{6,4},{7,5},{8,10},{9,11},{10,... | collective-permute-start | bytes 393224 | tf_op jit(solution)/shard_map/ppermute | solution.py:390
  63.7 12.5 %collective-permute-start.5 = (bf16[64,1024]{1,0:T(8,128)(2,1)S(1)}, bf16[64,1024]{1,0:T(8,128)(2,1)S(1)}, u32[]{:S(2)}, u32[]{:S(2)}) collective-permute-start(bf16[64,1024]{1,0:T(8,128)(2,1)S(1)} %get-tuple-element.56), channel_id=1, source_target_pairs={{0,3},{1,2},{2,1},{3,0},{4,7},{5,6},{6,5},{7,4},{8,11},{9,10},{10,... | collective-permute-start | bytes 393224 | tf_op jit(solution)/shard_map/ppermute | solution.py:390
  76.2 1.6 %collective-permute-start.6 = (bf16[128,1024]{1,0:T(8,128)(2,1)S(1)}, bf16[128,1024]{1,0:T(8,128)(2,1)S(1)}, u32[]{:S(2)}, u32[]{:S(2)}) collective-permute-start(bf16[128,1024]{1,0:T(8,128)(2,1)S(1)} %shard_map.74), channel_id=1, source_target_pairs={{0,4},{4,0},{8,12},{12,8},{16,20},{20,16},{24,28},{28,24},{1,5},{5... | collective-permute-start | bytes 786440 | tf_op jit(solution)/shard_map/ppermute | solution.py:390
  77.8 6.2 %collective-permute-start.7 = (bf16[64,1024]{1,0:T(8,128)(2,1)S(1)}, bf16[64,1024]{1,0:T(8,128)(2,1)S(1)}, u32[]{:S(2)}, u32[]{:S(2)}) collective-permute-start(bf16[64,1024]{1,0:T(8,128)(2,1)S(1)} %get-tuple-element.58), channel_id=1, source_target_pairs={{0,8},{4,12},{8,0},{12,4},{16,24},{20,28},{24,16},{28,20},{1,9},{5... | collective-permute-start | bytes 393224 | tf_op jit(solution)/shard_map/ppermute | solution.py:429
  79.2 8.1 %collective-permute-start.8 = (bf16[64,1024]{1,0:T(8,128)(2,1)S(1)}, bf16[64,1024]{1,0:T(8,128)(2,1)S(1)}, u32[]{:S(2)}, u32[]{:S(2)}) collective-permute-start(bf16[64,1024]{1,0:T(8,128)(2,1)S(1)} %get-tuple-element.59), channel_id=1, source_target_pairs={{0,16},{4,20},{8,24},{12,28},{16,0},{20,4},{24,8},{28,12},{1,17},{... | collective-permute-start | bytes 393224 | tf_op jit(solution)/shard_map/ppermute | solution.py:429
  80.7 6.6 %collective-permute-start.9 = (bf16[64,1024]{1,0:T(8,128)(2,1)S(1)}, bf16[64,1024]{1,0:T(8,128)(2,1)S(1)}, u32[]{:S(2)}, u32[]{:S(2)}) collective-permute-start(bf16[64,1024]{1,0:T(8,128)(2,1)S(1)} %get-tuple-element.60), channel_id=1, source_target_pairs={{0,24},{4,28},{8,16},{12,20},{16,8},{20,12},{24,0},{28,4},{1,25},{... | collective-permute-start | bytes 393224 | tf_op jit(solution)/shard_map/ppermute | solution.py:429
  94.6 10.0 %collective-permute-start.13 = (bf16[64,1024]{1,0:T(8,128)(2,1)S(1)}, bf16[64,1024]{1,0:T(8,128)(2,1)S(1)}, u32[]{:S(2)}, u32[]{:S(2)}) collective-permute-start(bf16[64,1024]{1,0:T(8,128)(2,1)S(1)} %get-tuple-element.66), channel_id=1, source_target_pairs={{0,24},{4,28},{8,16},{12,20},{16,8},{20,12},{24,0},{28,4},{1,25},{... | collective-permute-start | bytes 393224 | tf_op jit(solution)/shard_map/ppermute | solution.py:390
  96.1 8.8 %collective-permute-start.14 = (bf16[64,1024]{1,0:T(8,128)(2,1)S(1)}, bf16[64,1024]{1,0:T(8,128)(2,1)S(1)}, u32[]{:S(2)}, u32[]{:S(2)}) collective-permute-start(bf16[64,1024]{1,0:T(8,128)(2,1)S(1)} %get-tuple-element.67), channel_id=1, source_target_pairs={{0,28},{4,24},{8,20},{12,16},{16,12},{20,8},{24,4},{28,0},{1,29},{... | collective-permute-start | bytes 393224 | tf_op jit(solution)/shard_map/ppermute | solution.py:390
  96.1 10.1 %collective-permute-start.15 = (bf16[64,1024]{1,0:T(8,128)(2,1)S(1)}, bf16[64,1024]{1,0:T(8,128)(2,1)S(1)}, u32[]{:S(2)}, u32[]{:S(2)}) collective-permute-start(bf16[64,1024]{1,0:T(8,128)(2,1)S(1)} %get-tuple-element.68), channel_id=1, source_target_pairs={{0,8},{4,12},{8,0},{12,4},{16,24},{20,28},{24,16},{28,20},{1,9},{5... | collective-permute-start | bytes 393224 | tf_op jit(solution)/shard_map/ppermute | solution.py:390
  97.6 8.6 %collective-permute-start.16 = (bf16[64,1024]{1,0:T(8,128)(2,1)S(1)}, bf16[64,1024]{1,0:T(8,128)(2,1)S(1)}, u32[]{:S(2)}, u32[]{:S(2)}) collective-permute-start(bf16[64,1024]{1,0:T(8,128)(2,1)S(1)} %get-tuple-element.69), channel_id=1, source_target_pairs={{0,16},{4,20},{8,24},{12,28},{16,0},{20,4},{24,8},{28,12},{1,17},{... | collective-permute-start | bytes 393224 | tf_op jit(solution)/shard_map/ppermute | solution.py:390
  102.6 6.2 %collective-permute-start.17 = (bf16[64,1024]{1,0:T(8,128)(2,1)S(1)}, bf16[64,1024]{1,0:T(8,128)(2,1)S(1)}, u32[]{:S(2)}, u32[]{:S(2)}) collective-permute-start(bf16[64,1024]{1,0:T(8,128)(2,1)S(1)} %get-tuple-element.81), channel_id=1, source_target_pairs={{0,20},{4,16},{8,28},{12,24},{16,4},{20,0},{24,12},{28,8},{1,21},{... | collective-permute-start | bytes 393224 | tf_op jit(solution)/shard_map/ppermute | solution.py:390
  104.5 5.8 %collective-permute-start.18 = (bf16[64,1024]{1,0:T(8,128)(2,1)S(1)}, bf16[64,1024]{1,0:T(8,128)(2,1)S(1)}, u32[]{:S(2)}, u32[]{:S(2)}) collective-permute-start(bf16[64,1024]{1,0:T(8,128)(2,1)S(1)} %get-tuple-element.82), channel_id=1, source_target_pairs={{0,12},{4,8},{8,4},{12,0},{16,28},{20,24},{24,20},{28,16},{1,13},{... | collective-permute-start | bytes 393224 | tf_op jit(solution)/shard_map/ppermute | solution.py:390
  104.9 5.4 %collective-permute-start.19 = (bf16[64,1024]{1,0:T(8,128)(2,1)S(1)}, bf16[64,1024]{1,0:T(8,128)(2,1)S(1)}, u32[]{:S(2)}, u32[]{:S(2)}) collective-permute-start(bf16[64,1024]{1,0:T(8,128)(2,1)S(1)} %get-tuple-element.83), channel_id=1, source_target_pairs={{0,4},{4,0},{8,12},{12,8},{16,20},{20,16},{24,28},{28,24},{1,5},{5... | collective-permute-start | bytes 393224 | tf_op jit(solution)/shard_map/ppermute | solution.py:390
